TPU v7x, 256 devices: a whole 4x4x8 slice. The times are simulated.
256 devices in a mesh: tm: 32 (over z_lo, x, core), freq: 8 (over z_hi, y).
Axes of the slice: x: 4, y: 4, z: 8 (z_hi: 2, z_lo: 4; z = z_hi * 4 + z_lo), core: 2. Of those that a mesh axis runs over, the one named last changes fastest.
Arguments:
- visibilities: float32 [32, 8, 8, 512], P('tm', 'freq'), may hold values from -6 to 6
- coherency: bfloat16 [32, 8, 8, 64, 512], P('tm', 'freq'), may hold values from -0.75 to 0.75
- stations: int32 [32, 2, 512], P('tm'), may hold values from 0 to 511, as said below
- jones: float32 [8, 8, 32768], P('freq', None, 'tm'), may hold values from -3 to 3
- dual: float32 [8, 8, 32768], P('freq', None, 'tm'), may hold values from -1.8 to 1.8
- cluster: int32 [64], replicated, may hold values from 0 to 7
- rho_table: float32 [8], replicated, may hold values from 0.3 to 3
Outputs:
- jones_out: float32 [8, 8, 32768], P('freq', None, 'tm')
- dual_out: float32 [8, 8, 32768], P('freq', None, 'tm')
- consensus: float32 [3, 8, 32768], P(None, None, 'tm')
Inputs may be any that keep to these rules, and one draw needn't show every extreme that they name: Each baseline joins two different stations.
All inputs are finite; a program needn't handle non-finite values.
Results may differ from a plain program's by a relative error of at most 0.0003.
Values may be sent and summed in bfloat16 or wider, within the bound.
No kernel may reach another device: no remote copies, remote signals or barrier semaphores. Data moves between devices by JAX's collectives and lax.ppermute only.
A program may use at most 64 MiB of HBM per device.

v0:
```python
import functools
import math

import jax
import jax.numpy as jnp
import numpy as np
from jax import lax
from jax.experimental import pallas as pl
from jax.experimental.pallas import tpu as pltpu
from jax.sharding import Mesh
from jax.sharding import PartitionSpec as P

S = 512
K = 64
step_size = 0.5
epsilon = 1e-06


f32 = jnp.float32
bf16 = jnp.bfloat16


def poly_basis(channels, degrees):
    points = np.linspace(-1.0, 1.0, channels)
    columns = []
    for degree in range(degrees):
        column = points**degree
        for earlier in columns:
            column = column - np.dot(earlier, column) * earlier
        column = column / np.sqrt(np.dot(column, column))
        columns.append(column)
    return np.stack(columns, axis=1).astype(np.float32)


def swap(value, axis, mask):
    size = {"tm": 32, "zh": 2, "y": 4}[axis]
    return lax.ppermute(value, axis, [(i, i ^ mask) for i in range(size)])


def spread(value):
    own = jnp.concatenate([value] + [swap(value, "tm", 8 * d) for d in (1, 2, 3)], axis=0)
    return own, swap(own, "tm", 1)


def collect(own, other):
    line = (own + swap(other, "tm", 1)).reshape(4, 64, 128)
    parts = [line[0]] + [swap(line[d], "tm", 8 * d) for d in (1, 2, 3)]
    return (parts[0] + parts[1]) + (parts[2] + parts[3])


def pair_times(a, b):
    return (a[0] * b[0] - a[1] * b[1], a[0] * b[1] + a[1] * b[0])


def pair_times_conj(a, b):
    return (a[0] * b[0] + a[1] * b[1], a[1] * b[0] - a[0] * b[1])


def pair_conj_times(a, b):
    return (a[0] * b[0] + a[1] * b[1], a[0] * b[1] - a[1] * b[0])


def pair_add(a, b):
    return (a[0] + b[0], a[1] + b[1])


def matrix(parts):
    return [[(parts[0], parts[1]), (parts[2], parts[3])], [(parts[4], parts[5]), (parts[6], parts[7])]]


def flat(m):
    return [m[0][0][0], m[0][0][1], m[0][1][0], m[0][1][1], m[1][0][0], m[1][0][1], m[1][1][0], m[1][1][1]]


def times(a, b):
    return [[pair_add(pair_times(a[i][0], b[0][j]), pair_times(a[i][1], b[1][j])) for j in range(2)] for i in range(2)]


def times_h(a, b):
    return [
        [pair_add(pair_times_conj(a[i][0], b[j][0]), pair_times_conj(a[i][1], b[j][1])) for j in range(2)]
        for i in range(2)
    ]


def h_times(a, b):
    return [
        [pair_add(pair_conj_times(a[0][i], b[0][j]), pair_conj_times(a[1][i], b[1][j])) for j in range(2)]
        for i in range(2)
    ]


def split(value):
    high = value.astype(bf16)
    return high, (value - high.astype(f32)).astype(bf16)


VMEM = pl.BlockSpec(memory_space=pltpu.VMEM)


def call(body, outs, scratch, args, aliases=None, smem=0):
    return pl.pallas_call(
        body,
        out_shape=[jax.ShapeDtypeStruct(*o) for o in outs],
        in_specs=[pl.BlockSpec(memory_space=pltpu.SMEM)] * smem + [VMEM] * (len(args) - smem),
        out_specs=[VMEM] * len(outs),
        scratch_shapes=[pltpu.VMEM(*b) for b in scratch],
        compiler_params=pltpu.CompilerParams(vmem_limit_bytes=28 << 20),
        input_output_aliases=aliases or {},
    )(*args)


def last_kernel(degrees, near0, near1, near2, near3, basis, current, dual, rho, out, dual_out, poly):
    fitted = None
    for j in range(degrees):
        sums = []
        for half in range(2):
            rows = slice(half * 64, half * 64 + 64)
            terms = [
                basis[half * 4 + d : half * 4 + d + 1, j : j + 1] * ref[rows, :]
                for d, ref in enumerate((near0, near1, near2, near3))
            ]
            sums.append((terms[0] + terms[1]) + (terms[2] + terms[3]))
        coefficient = sums[0] + sums[1]
        poly[j * 64 : j * 64 + 64, :] = coefficient
        term = basis[0:1, j : j + 1] * coefficient
        fitted = term if fitted is None else fitted + term
    out[...] = current[...]
    dual_out[...] = dual[...] + rho[...] * (current[...] - fitted)


def step_kernel(count, zh, squares, value, down, far_value, far_down, current, pair, out):
    owner = lax.broadcasted_iota(jnp.int32, (64, 128), 0) & 1
    steps = []
    for side in (zh[0], 1 - zh[0]):
        kept = jnp.where(owner == side, squares[...], 0.0)
        total = jnp.sum(jnp.sum(kept, axis=0, keepdims=True), axis=1, keepdims=True)
        steps.append(step_size / jnp.sqrt(total / count + epsilon))
    pair[0:64, :] = value[...] - steps[0] * down[...]
    pair[64:128, :] = far_value[...] - steps[1] * far_down[...]
    out[...] = current[...] - steps[0] * down[...]


def stations_of(sky):
    rows = sky[128:144, :].astype(f32)
    return [rows[2 * side : 2 * side + 1] * 16.0 + rows[2 * side + 1 : 2 * side + 2] for side in range(2)]


def place_table_kernel(sky0, sky1, sky2, sky3, after, out):
    station = lax.broadcasted_iota(jnp.int32, (512, 512), 1).astype(f32)
    rows = [row for sky in (sky0, sky1, sky2, sky3) for row in stations_of(sky)]
    columns = jnp.concatenate(rows, axis=0).T
    for j in range(8):
        hit = station == columns[:, j : j + 1]
        out[j * 512 : j * 512 + 512, :] = jnp.where(hit, 1.0, 0.0).astype(bf16)


def sky_kernel(tm, coherency, stations, *outs):
    slot = lax.broadcasted_iota(jnp.int32, (64, 64), 0)
    owner = tm[0] ^ ((slot & 3) * 8 + (slot >> 4) * 2 + ((slot >> 2) & 1))
    order = owner * 2 + ((slot >> 3) & 1) == lax.broadcasted_iota(jnp.int32, (64, 64), 1)
    order = jnp.where(order, 1.0, 0.0).astype(bf16)
    for c in range(8):
        rows = jnp.dot(order, coherency[c], preferred_element_type=f32).astype(bf16)
        for d in range(4):
            outs[d][c * 16 : c * 16 + 16, :] = rows[d * 16 : d * 16 + 16, :]
    ids = stations[...]
    parts = [part for side in range(2) for part in (ids[side : side + 1] >> 4, ids[side : side + 1] & 15)]
    rows = jnp.concatenate(parts + [jnp.zeros((12, 512), jnp.int32)], axis=0).astype(f32).astype(bf16)
    for d in range(4):
        outs[d][128:144, :] = rows


def pick_kernel(own, other, sky0, sky1, sky2, sky3, gains, stage, lhs, table):
    stage[0:256, :] = own[...]
    stage[256:512, :] = other[...]
    for c in range(8):
        for block in range(4):
            first = stage[pl.ds(block * 8 + c, 8, stride=64), :]
            second = stage[pl.ds(block * 8 + 32 + c, 8, stride=64), :]
            high, low = split(jnp.concatenate([first, second], axis=0))
            lanes = slice(block * 128, block * 128 + 128)
            lhs[c * 16 : c * 16 + 16, lanes] = high
            lhs[128 + c * 16 : 144 + c * 16, lanes] = low
    station = lax.broadcasted_iota(jnp.int32, (512, 512), 0).astype(f32)
    for s, sky in enumerate((sky0, sky1, sky2, sky3)):
        for side, row in enumerate(stations_of(sky)):
            hit = station == row
            table[s % 2, :, side * 512 : side * 512 + 512] = jnp.where(hit, 1.0, 0.0).astype(bf16)
        both = jnp.dot(lhs[...], table[s % 2], preferred_element_type=f32)
        gains[:, s * 1024 : s * 1024 + 1024] = both[0:128] + both[128:256]


def halves(ref, c, lanes):
    rows = ref[c * 16 : c * 16 + 16, lanes].astype(f32)
    return rows[0:8], rows[8:16]


def model_kernel(count, moved, *refs):
    if moved:
        before, delta, n0, n1, n2, n3, sky0, sky1, sky2, sky3, vis, gains, part, rate = refs
        total = (n0[...] + n1[...]) + (n2[...] + n3[...])
        mean = jnp.sum(total, axis=(0, 1), keepdims=True) / count
        step = jnp.broadcast_to(step_size / jnp.sqrt(mean + epsilon), (8, 128))
        rate[...] = step
    else:
        gains, sky0, sky1, sky2, sky3, vis, part = refs
    for s, sky in enumerate((sky0, sky1, sky2, sky3)):

        def block(nb, carry, s=s, sky=sky):
            def at(base):
                return pl.ds(pl.multiple_of(base + nb * 128, 128), 128)

            here, plane, qlane = at(0), at(s * 1024), at(s * 1024 + 512)
            models = [halves(sky, c, here) for c in range(8)]
            sums = None
            for h in range(2):
                ends = []
                for lanes in (plane, qlane):
                    values = []
                    for c in range(8):
                        rows = slice(c * 16 + h * 8, c * 16 + h * 8 + 8)
                        if moved:
                            value = before[rows, lanes] - step * delta[rows, lanes]
                            gains[rows, lanes] = value
                        else:
                            value = gains[rows, lanes]
                        values.append(value)
                    ends.append(matrix(values))
                product = times(ends[0], matrix([m[h] for m in models]))
                result = flat(times_h(product, ends[1]))
                sums = result if sums is None else [a + b for a, b in zip(sums, result)]
            for c in range(8):
                row = jnp.sum(sums[c], axis=0, keepdims=True)
                if s == 0:
                    row = row - vis[c : c + 1, here]
                part[s * 8 + c : s * 8 + c + 1, here] = row
            return carry

        lax.fori_loop(0, 4, block, 0)


def terms_kernel(weight, part, r1, r2, r3, gains, sky0, sky1, sky2, sky3, place, gown, gother, terms, stage):
    for s, sky in enumerate((sky0, sky1, sky2, sky3)):

        def block(nb, carry, s=s, sky=sky):
            def at(base):
                return pl.ds(pl.multiple_of(base + nb * 128, 128), 128)

            def slot(ref, t):
                return ref[t * 8 : t * 8 + 8, at(0)]

            error = (slot(part, s) + slot(r1, s ^ 1)) + (slot(r2, s ^ 2) + slot(r3, s ^ 3))
            error = error * weight
            errors = matrix([jnp.broadcast_to(error[c : c + 1], (8, 128)) for c in range(8)])
            models = [halves(sky, c, at(0)) for c in range(8)]
            outs = ([], [])
            for h in range(2):
                rows = [slice(c * 16 + h * 8, c * 16 + h * 8 + 8) for c in range(8)]
                model = matrix([m[h] for m in models])
                second = matrix([gains[r, at(s * 1024 + 512)] for r in rows])
                outs[0].append(flat(times(errors, times_h(second, model))))
                first = matrix([gains[r, at(s * 1024)] for r in rows])
                outs[1].append(flat(h_times(errors, times(first, model))))
            for side in range(2):
                lanes = at(s * 1024 + side * 512)
                for c in range(8):
                    high, low = split(jnp.concatenate([outs[side][0][c], outs[side][1][c]], axis=0))
                    terms[c * 16 : c * 16 + 16, lanes] = high
                    terms[128 + c * 16 : 144 + c * 16, lanes] = low
            return carry

        lax.fori_loop(0, 4, block, 0)
    both = jnp.dot(terms[...], place[...], preferred_element_type=f32)
    sums = both[0:128] + both[128:256]
    for c in range(8):
        for block in range(8):
            row = c * 16 + block // 4 * 8
            lane = block % 4 * 128
            stage[pl.ds(block * 8 + c, 8, stride=64), :] = sums[row : row + 8, lane : lane + 128]
    gown[...] = stage[0:256, :]
    gother[...] = stage[256:512, :]


def body(visibilities, coherency, stations, jones, dual, cluster, rho_table):
    channels = lax.axis_size("zh") * lax.axis_size("y")
    degrees = min(3, channels - 1)
    tm = lax.axis_index("tm")
    zh = lax.axis_index("zh")
    freq = zh * 4 + lax.axis_index("y")
    weight = np.float32(math.sqrt(S / (2.0 * lax.axis_size("tm") * visibilities.shape[3])))
    count = 8.0 * K * S

    def packed(value):
        return value.reshape(8, 8, 128).transpose(1, 0, 2).reshape(64, 128)

    def unpacked(value):
        return value.reshape(-1, 8, 8, 128).transpose(0, 2, 1, 3).reshape(-1, 8, 1024)

    start = packed(jones[0])
    dual_start = packed(dual[0])
    rho_dir = jnp.sum(
        jnp.where(cluster[:, None] == jnp.arange(rho_table.shape[0], dtype=jnp.int32)[None, :], rho_table[None, :], 0.0),
        axis=1,
    )
    rho = jnp.repeat(lax.dynamic_slice_in_dim(rho_dir, tm * 2, 2), 32)[:, None]
    table = jnp.asarray(poly_basis(channels, degrees))
    basis = [lax.dynamic_index_in_dim(table, freq ^ d, 0, keepdims=False) for d in range(8)]

    def y_line(value):
        return [value] + [swap(value, "y", d) for d in (1, 2, 3)]

    def consensus_of(value):
        pair = jnp.stack([value, swap(value, "zh", 1)])
        parts = y_line(pair)
        sums = []
        for half in range(2):
            rows = basis[half * 4 : half * 4 + 4]
            terms = [b.reshape((-1,) + (1,) * value.ndim) * v[half][None] for b, v in zip(rows, parts)]
            sums.append((terms[0] + terms[1]) + (terms[2] + terms[3]))
        return sums[0] + sums[1]

    def project(poly):
        return jnp.sum(basis[0][:, None, None] * poly, axis=0)

    own, other = spread(start)
    args = (tm.astype(jnp.int32).reshape(1), coherency[0, 0], stations[0])
    skies = call(sky_kernel, [((144, 512), bf16)] * 4, [], args, smem=1)
    skies = [skies[0]] + [swap(skies[d], "tm", 2 * d) for d in (1, 2, 3)]
    vis = visibilities[0, 0]
    many = ((128, 4096), f32)
    model_outs = [((32, 512), f32)]

    def gains_of(own, other):
        scratch = [((512, 128), f32), ((256, 512), bf16), ((2, 512, 1024), bf16)]
        return call(pick_kernel, [many], scratch, (own, other, *skies))[0]

    def gradient_of(gains, part):
        others = [swap(part, "tm", 2 * d) for d in (1, 2, 3)]
        outs = [((256, 128), f32)] * 2
        scratch = [((256, 4096), bf16), ((512, 128), f32)]
        place = call(place_table_kernel, [((4096, 512), bf16)], [], (*skies, part))[0]
        args = (part, *others, gains, *skies, place)
        return collect(*call(functools.partial(terms_kernel, weight), outs, scratch, args))

    gains = gains_of(own, other)
    (part,) = call(functools.partial(model_kernel, count, False), model_outs, [], (gains, *skies, vis))

    fitted = project(consensus_of(start + dual_start / rho))
    descent = gradient_of(gains, part) + dual_start + rho * (start - fitted)

    down, dother = spread(descent)
    norm = jnp.sum((down * down + dother * dother).reshape(32, 8, 128), axis=0)
    norms = [norm] + [swap(norm, "tm", 2 * d) for d in (1, 2, 3)]
    delta = gains_of(down, dother)
    gains, part, rate = call(
        functools.partial(model_kernel, count, True),
        [many] + model_outs + [((8, 128), f32)],
        [],
        (gains, delta, *norms, *skies, vis),
        {0: 0},
    )
    current = start - rate[0:1, :] * descent
    fitted = project(consensus_of(current + dual_start / rho))
    dual_now = dual_start + rho * (current - fitted)

    descent = gradient_of(gains, part) + dual_now + rho * (current - fitted)
    near = jnp.stack([current + dual_now / rho, descent])
    far = swap(near, "zh", 1)
    squares = jnp.sum((descent * descent).reshape(64, 128), axis=0)[None, None, :]
    squares = lax.all_to_all(jnp.broadcast_to(squares, (64, 1, 128)), ("tm", "zh"), 0, 0, tiled=True).reshape(64, 128)
    args = (zh.astype(jnp.int32).reshape(1), squares, near[0], near[1], far[0], far[1], current)
    outs = [((128, 128), f32), ((64, 128), f32)]
    pair, current = call(functools.partial(step_kernel, count), outs, [], args, smem=1)
    lines = y_line(pair)
    rows = jnp.zeros((8, 128), f32).at[:, :degrees].set(jnp.stack(basis))
    args = (*lines, rows, current, dual_now, jnp.broadcast_to(rho, (64, 128)))
    outs = [((64, 128), f32), ((64, 128), f32), ((degrees * 64, 128), f32)]
    current, dual_now, poly = call(functools.partial(last_kernel, degrees), outs, [], args)
    return unpacked(current), unpacked(dual_now), unpacked(poly)


def solution(mesh):
    fine = Mesh(mesh.devices.reshape(32, 2, 4), ("tm", "zh", "y"))
    freq = ("zh", "y")

    return jax.shard_map(
        body,
        mesh=fine,
        in_specs=(
            P("tm", freq, None, None),
            P("tm", freq, None, None, None),
            P("tm", None, None),
            P(freq, None, "tm"),
            P(freq, None, "tm"),
            P(),
            P(),
        ),
        out_specs=(P(freq, None, "tm"), P(freq, None, "tm"), P(None, None, "tm")),
        check_vma=False,
    )
```

profile of v0, /device:TPU:2, one launch (start us, length us, event | category | flops | bytes accessed | tf_op | source)
XLA Modules:
  0.0 133.3 jit_solution(4763624245297155535)
XLA Ops:
  0.6 2.0 %collective-permute-start = (f32[64,128]{1,0:T(8,128)}, f32[64,128]{1,0:T(8,128)S(1)}, u32[]{:S(2)}, u32[]{:S(2)}) collective-permute-start(f32[64,128]{1,0:T(8,128)} %bitcast.111), channel_id=1, source_target_pairs={{0,64},{8,72},{16,80},{24,88},{32,96},{40,104},{48,112},{56,120},{... | collective-permute-start | bytes 98312 | tf_op jit(solution)/shard_map/ppermute | solution.py:37
  2.6 3.3 %collective-permute-start.1 = (f32[64,128]{1,0:T(8,128)}, f32[64,128]{1,0:T(8,128)S(1)}, u32[]{:S(2)}, u32[]{:S(2)}) collective-permute-start(f32[64,128]{1,0:T(8,128)} %bitcast.112), channel_id=1, source_target_pairs={{0,128},{8,136},{16,144},{24,152},{32,160},{40,168},{48,176},{56,1... | collective-permute-start | bytes 98312 | tf_op jit(solution)/shard_map/ppermute | solution.py:37
  5.9 1.0 copy-done
  7.0 0.7 copy-done.2
  7.9 1.5 %collective-permute-start.4 = (bf16[144,512]{1,0:T(8,128)(2,1)S(1)}, bf16[144,512]{1,0:T(8,128)(2,1)S(1)}, u32[]{:S(2)}, u32[]{:S(2)}) collective-permute-start(bf16[144,512]{1,0:T(8,128)(2,1)S(1)} %get-tuple-element.32), channel_id=1, source_target_pairs={{0,16},{8,24},{16,0},{24,8},{32,48},{40,56},{48,32},{56,40},{64,80... | collective-permute-start | bytes 442376 | tf_op jit(solution)/shard_map/ppermute | solution.py:37
  9.4 0.8 select_reduce_fusion
  10.4 0.9 fusion.8
  11.3 5.6 %collective-permute-start.14 = (f32[64,128]{1,0:T(8,128)S(1)}, f32[64,128]{1,0:T(8,128)S(1)}, u32[]{:S(2)}, u32[]{:S(2)}) collective-permute-start(f32[64,128]{1,0:T(8,128)S(1)} %fusion.8), channel_id=1, source_target_pairs={{0,4},{4,0},{1,5},{5,1},{2,6},{6,2},{3,7},{7,3},{8,12},{12,8},{9,1... | collective-permute-start | bytes 98312 | tf_op jit(solution)/shard_map/ppermute | solution.py:37
  16.9 0.9 fusion.6
  17.8 1.0 constant_dynamic-slice_fusion
  18.8 0.4 collective-permute-done.14
  19.2 2.1 %collective-permute-start.5 = (bf16[144,512]{1,0:T(8,128)(2,1)S(1)}, bf16[144,512]{1,0:T(8,128)(2,1)S(1)}, u32[]{:S(2)}, u32[]{:S(2)}) collective-permute-start(bf16[144,512]{1,0:T(8,128)(2,1)S(1)} %get-tuple-element.33), channel_id=1, source_target_pairs={{0,32},{8,40},{16,48},{24,56},{32,0},{40,8},{48,16},{56,24},{64,96... | collective-permute-start | bytes 442376 | tf_op jit(solution)/shard_map/ppermute | solution.py:37
  21.3 0.6 collective-permute-start.6
  21.9 1.6 %collective-permute-start.15 = (f32[2,64,128]{2,1,0:T(8,128)S(1)}, f32[2,64,128]{2,1,0:T(8,128)S(1)}, u32[]{:S(2)}, u32[]{:S(2)}) collective-permute-start(f32[2,64,128]{2,1,0:T(8,128)S(1)} %pad_maximum_fusion.2), channel_id=1, source_target_pairs={{0,1},{1,0},{2,3},{3,2},{4,5},{5,4},{6,7},{7,6},{8,9},{9,8},{10,11... | collective-permute-start | bytes 196616 | tf_op jit(solution)/shard_map/ppermute | solution.py:37
  23.5 2.9 %collective-permute-start.16 = (f32[2,64,128]{2,1,0:T(8,128)S(1)}, f32[2,64,128]{2,1,0:T(8,128)S(1)}, u32[]{:S(2)}, u32[]{:S(2)}) collective-permute-start(f32[2,64,128]{2,1,0:T(8,128)S(1)} %pad_maximum_fusion.2), channel_id=1, source_target_pairs={{0,2},{1,3},{2,0},{3,1},{4,6},{5,7},{6,4},{7,5},{8,10},{9,11},{10,... | collective-permute-start | bytes 196616 | tf_op jit(solution)/shard_map/ppermute | solution.py:37
  26.4 0.8 pad_maximum_fusion.own
  27.3 2.0 %collective-permute-start.17 = (f32[2,64,128]{2,1,0:T(8,128)S(1)}, f32[2,64,128]{2,1,0:T(8,128)S(1)}, u32[]{:S(2)}, u32[]{:S(2)}) collective-permute-start(f32[2,64,128]{2,1,0:T(8,128)S(1)} %pad_maximum_fusion.2), channel_id=1, source_target_pairs={{0,3},{1,2},{2,1},{3,0},{4,7},{5,6},{6,5},{7,4},{8,11},{9,10},{10,... | collective-permute-start | bytes 196616 | tf_op jit(solution)/shard_map/ppermute | solution.py:37
  29.3 1.4 %shard_map.104.refs_0_.gains = f32[128,4096]{1,0:T(8,128)S(1)} custom-call(f32[256,128]{1,0:T(8,128)S(1)} %pad_maximum_fusion.own, f32[256,128]{1,0:T(8,128)S(1)} %collective-permute-done.3.other, bf16[144,512]{1,0:T(8,128)(2,1)S(1)} %get-tuple-element.31.sky0.refs_1_.refs_6_, bf16[144,512]{1,0:T(8,128)(2,1)S(1)} %collective-permute-done.4.sky1.refs_2_.refs_7_, ...), custom_call_target="tpu_custom_call" | custom-call | tf_op jit(solution)/shard_map/pallas_call | solution.py:102
  30.7 0.8 shard_map.105.after.part
  31.6 1.8 %collective-permute-start.7 = (f32[32,512]{1,0:T(8,128)S(1)}, f32[32,512]{1,0:T(8,128)S(1)}, u32[]{:S(2)}, u32[]{:S(2)}) collective-permute-start(f32[32,512]{1,0:T(8,128)S(1)} %shard_map.105.after.part), channel_id=1, source_target_pairs={{0,16},{8,24},{16,0},{24,8},{32,48},{40,56},{48,32},{56,40},{64,80... | collective-permute-start | bytes 196616 | tf_op jit(solution)/shard_map/ppermute | solution.py:37
  33.4 1.7 %collective-permute-start.8 = (f32[32,512]{1,0:T(8,128)S(1)}, f32[32,512]{1,0:T(8,128)S(1)}, u32[]{:S(2)}, u32[]{:S(2)}) collective-permute-start(f32[32,512]{1,0:T(8,128)S(1)} %shard_map.105.after.part), channel_id=1, source_target_pairs={{0,32},{8,40},{16,48},{24,56},{32,0},{40,8},{48,16},{56,24},{64,96... | collective-permute-start | bytes 196616 | tf_op jit(solution)/shard_map/ppermute | solution.py:37
  35.1 0.5 collective-permute-start.9
  35.6 0.9 shard_map.106.place
  36.5 2.7 %collective-permute-done.8.r2 = f32[32,512]{1,0:T(8,128)S(1)} collective-permute-done((f32[32,512]{1,0:T(8,128)S(1)}, f32[32,512]{1,0:T(8,128)S(1)}, u32[]{:S(2)}, u32[]{:S(2)}) %collective-permute-start.8) | collective-permute-done | bytes 65568 | tf_op jit(solution)/shard_map/ppermute | solution.py:37
  39.2 1.1 collective-permute-done.9.r3
  40.3 3.0 %shard_map.107 = (f32[256,128]{1,0:T(8,128)S(1)}, f32[256,128]{1,0:T(8,128)S(1)}) custom-call(f32[32,512]{1,0:T(8,128)S(1)} %shard_map.105.after.part, f32[32,512]{1,0:T(8,128)S(1)} %collective-permute-done.7.r1, f32[32,512]{1,0:T(8,128)S(1)} %collective-permute-done.8.r2, f32[32,512]{1,0:T(8,128)S(1)} %collective-permute-done.9.r3, ...), custom_call_target="tpu_custom_call" | custom-call | tf_op jit(solution)/shard_map/pallas_call | solution.py:102
  43.6 1.3 collective-permute-done.10
  45.2 3.9 %collective-permute-start.12 = (f32[64,128]{1,0:T(8,128)S(1)}, f32[64,128]{1,0:T(8,128)S(1)}, u32[]{:S(2)}, u32[]{:S(2)}) collective-permute-start(f32[64,128]{1,0:T(8,128)S(1)} %get-tuple-element.57), channel_id=1, source_target_pairs={{0,128},{8,136},{16,144},{24,152},{32,160},{40,168},{48,176},{56,1... | collective-permute-start | bytes 98312 | tf_op jit(solution)/shard_map/ppermute | solution.py:37
  49.6 1.4 %collective-permute-done.12 = f32[64,128]{1,0:T(8,128)S(1)} collective-permute-done((f32[64,128]{1,0:T(8,128)S(1)}, f32[64,128]{1,0:T(8,128)S(1)}, u32[]{:S(2)}, u32[]{:S(2)}) %collective-permute-start.12) | collective-permute-done | bytes 32800 | tf_op jit(solution)/shard_map/ppermute | solution.py:37
  51.0 3.8 %collective-permute-done.13 = f32[64,128]{1,0:T(8,128)S(1)} collective-permute-done((f32[64,128]{1,0:T(8,128)S(1)}, f32[64,128]{1,0:T(8,128)S(1)}, u32[]{:S(2)}, u32[]{:S(2)}) %collective-permute-start.13) | collective-permute-done | bytes 32800 | tf_op jit(solution)/shard_map/ppermute | solution.py:37
  54.9 0.9 collective-permute-start.19
  55.8 3.5 %collective-permute-start.20 = (f32[64,128]{1,0:T(8,128)S(1)}, f32[64,128]{1,0:T(8,128)S(1)}, u32[]{:S(2)}, u32[]{:S(2)}) collective-permute-start(f32[64,128]{1,0:T(8,128)S(1)} %fusion.5), channel_id=1, source_target_pairs={{0,192},{8,200},{16,208},{24,216},{32,224},{40,232},{48,240},{56,2... | collective-permute-start | bytes 98312 | tf_op jit(solution)/shard_map/ppermute | solution.py:37
  59.3 0.5 collective-permute-done.19
  59.8 1.7 %collective-permute-done.20 = f32[64,128]{1,0:T(8,128)S(1)} collective-permute-done((f32[64,128]{1,0:T(8,128)S(1)}, f32[64,128]{1,0:T(8,128)S(1)}, u32[]{:S(2)}, u32[]{:S(2)}) %collective-permute-start.20) | collective-permute-done | bytes 32800 | tf_op jit(solution)/shard_map/ppermute | solution.py:37
  61.7 1.3 %collective-permute-done.21.other = f32[256,128]{1,0:T(8,128)S(1)} collective-permute-done((f32[256,128]{1,0:T(8,128)S(1)}, f32[256,128]{1,0:T(8,128)S(1)}, u32[]{:S(2)}, u32[]{:S(2)}) %collective-permute-start.21) | collective-permute-done | bytes 131104 | tf_op jit(solution)/shard_map/ppermute | solution.py:37
  63.0 2.9 %collective-permute-start.22 = (f32[8,128]{1,0:T(8,128)S(1)}, f32[8,128]{1,0:T(8,128)S(1)}, u32[]{:S(2)}, u32[]{:S(2)}) collective-permute-start(f32[8,128]{1,0:T(8,128)S(1)} %bitcast_reduce_fusion.refs_2_), channel_id=1, source_target_pairs={{0,16},{8,24},{16,0},{24,8},{32,48},{40,56},{48,32},{56,40},{64,80... | collective-permute-start | bytes 12296 | tf_op jit(solution)/shard_map/ppermute | solution.py:37
  65.9 1.6 %collective-permute-start.24 = (f32[8,128]{1,0:T(8,128)S(1)}, f32[8,128]{1,0:T(8,128)S(1)}, u32[]{:S(2)}, u32[]{:S(2)}) collective-permute-start(f32[8,128]{1,0:T(8,128)S(1)} %bitcast_reduce_fusion.refs_2_), channel_id=1, source_target_pairs={{0,48},{8,56},{16,32},{24,40},{32,16},{40,24},{48,0},{56,8},{64,11... | collective-permute-start | bytes 12296 | tf_op jit(solution)/shard_map/ppermute | solution.py:37
  67.5 1.4 %shard_map.108.refs_1_ = f32[128,4096]{1,0:T(8,128)S(1)} custom-call(f32[256,128]{1,0:T(8,128)S(1)} %pad_maximum_fusion.1.own, f32[256,128]{1,0:T(8,128)S(1)} %collective-permute-done.21.other, bf16[144,512]{1,0:T(8,128)(2,1)S(1)} %get-tuple-element.31.sky0.refs_1_.refs_6_, bf16[144,512]{1,0:T(8,128)(2,1)S(1)} %collective-permute-done.4.sky1.refs_2_.refs_7_, ...), custom_call_target="tpu_custom_call" | custom-call | tf_op jit(solution)/shard_map/pallas_call | solution.py:102
  68.9 2.2 %collective-permute-done.23.refs_4_ = f32[8,128]{1,0:T(8,128)S(1)} collective-permute-done((f32[8,128]{1,0:T(8,128)S(1)}, f32[8,128]{1,0:T(8,128)S(1)}, u32[]{:S(2)}, u32[]{:S(2)}) %collective-permute-start.23) | collective-permute-done | bytes 4128 | tf_op jit(solution)/shard_map/ppermute | solution.py:37
  71.1 2.0 %shard_map.109 = (f32[128,4096]{1,0:T(8,128)S(1)}, f32[32,512]{1,0:T(8,128)S(1)}, f32[8,128]{1,0:T(8,128)S(1)}) custom-call(f32[128,4096]{1,0:T(8,128)S(1)} %shard_map.104.refs_0_.gains, f32[128,4096]{1,0:T(8,128)S(1)} %shard_map.108.refs_1_, f32[8,128]{1,0:T(8,128)S(1)} %bitcast_reduce_fusion.refs_2_, ...), custom_call_target="tpu_custom_call", output_to_operand_aliasing={{0}: (0, {})} | custom-call | tf_op jit(solution)/shard_map/pallas_call | solution.py:102
  73.2 5.9 %collective-permute-start.32 = (f32[64,128]{1,0:T(8,128)S(1)}, f32[64,128]{1,0:T(8,128)S(1)}, u32[]{:S(2)}, u32[]{:S(2)}) collective-permute-start(f32[64,128]{1,0:T(8,128)S(1)} %get-tuple-element.51), channel_id=1, source_target_pairs={{0,4},{4,0},{1,5},{5,1},{2,6},{6,2},{3,7},{7,3},{8,12},{12,8},{9,1... | collective-permute-start | bytes 98312 | tf_op jit(solution)/shard_map/ppermute | solution.py:37
  79.1 1.6 %collective-permute-start.25 = (f32[32,512]{1,0:T(8,128)S(1)}, f32[32,512]{1,0:T(8,128)S(1)}, u32[]{:S(2)}, u32[]{:S(2)}) collective-permute-start(f32[32,512]{1,0:T(8,128)S(1)} %get-tuple-element.37.after.part), channel_id=1, source_target_pairs={{0,16},{8,24},{16,0},{24,8},{32,48},{40,56},{48,32},{56,40},{64,80... | collective-permute-start | bytes 196616 | tf_op jit(solution)/shard_map/ppermute | solution.py:37
  80.7 1.6 %collective-permute-start.26 = (f32[32,512]{1,0:T(8,128)S(1)}, f32[32,512]{1,0:T(8,128)S(1)}, u32[]{:S(2)}, u32[]{:S(2)}) collective-permute-start(f32[32,512]{1,0:T(8,128)S(1)} %get-tuple-element.37.after.part), channel_id=1, source_target_pairs={{0,32},{8,40},{16,48},{24,56},{32,0},{40,8},{48,16},{56,24},{64,96... | collective-permute-start | bytes 196616 | tf_op jit(solution)/shard_map/ppermute | solution.py:37
  82.3 0.6 collective-permute-start.27
  83.1 0.9 shard_map.110.place
  84.0 2.7 %collective-permute-start.34 = (f32[2,64,128]{2,1,0:T(8,128)S(1)}, f32[2,64,128]{2,1,0:T(8,128)S(1)}, u32[]{:S(2)}, u32[]{:S(2)}) collective-permute-start(f32[2,64,128]{2,1,0:T(8,128)S(1)} %pad_maximum_fusion.3), channel_id=1, source_target_pairs={{0,2},{1,3},{2,0},{3,1},{4,6},{5,7},{6,4},{7,5},{8,10},{9,11},{10,... | collective-permute-start | bytes 196616 | tf_op jit(solution)/shard_map/ppermute | solution.py:37
  86.8 1.9 %collective-permute-start.35 = (f32[2,64,128]{2,1,0:T(8,128)S(1)}, f32[2,64,128]{2,1,0:T(8,128)S(1)}, u32[]{:S(2)}, u32[]{:S(2)}) collective-permute-start(f32[2,64,128]{2,1,0:T(8,128)S(1)} %pad_maximum_fusion.3), channel_id=1, source_target_pairs={{0,3},{1,2},{2,1},{3,0},{4,7},{5,6},{6,5},{7,4},{8,11},{9,10},{10,... | collective-permute-start | bytes 196616 | tf_op jit(solution)/shard_map/ppermute | solution.py:37
  88.7 3.0 %shard_map.111 = (f32[256,128]{1,0:T(8,128)S(1)}, f32[256,128]{1,0:T(8,128)S(1)}) custom-call(f32[32,512]{1,0:T(8,128)S(1)} %get-tuple-element.37.after.part, f32[32,512]{1,0:T(8,128)S(1)} %collective-permute-done.25.r1, f32[32,512]{1,0:T(8,128)S(1)} %collective-permute-done.26.r2, f32[32,512]{1,0:T(8,128)S(1)} %collective-permute-done.27.r3, ...), custom_call_target="tpu_custom_call" | custom-call | tf_op jit(solution)/shard_map/pallas_call | solution.py:102
  92.4 0.8 collective-permute-done.28
  93.3 2.5 %collective-permute-start.30 = (f32[64,128]{1,0:T(8,128)S(1)}, f32[64,128]{1,0:T(8,128)S(1)}, u32[]{:S(2)}, u32[]{:S(2)}) collective-permute-start(f32[64,128]{1,0:T(8,128)S(1)} %get-tuple-element.55), channel_id=1, source_target_pairs={{0,128},{8,136},{16,144},{24,152},{32,160},{40,168},{48,176},{56,1... | collective-permute-start | bytes 98312 | tf_op jit(solution)/shard_map/ppermute | solution.py:37
  95.8 1.9 %collective-permute-start.31 = (f32[64,128]{1,0:T(8,128)S(1)}, f32[64,128]{1,0:T(8,128)S(1)}, u32[]{:S(2)}, u32[]{:S(2)}) collective-permute-start(f32[64,128]{1,0:T(8,128)S(1)} %get-tuple-element.54), channel_id=1, source_target_pairs={{0,192},{8,200},{16,208},{24,216},{32,224},{40,232},{48,240},{56,2... | collective-permute-start | bytes 98312 | tf_op jit(solution)/shard_map/ppermute | solution.py:37
  97.8 1.0 collective-permute-done.30
  98.8 2.7 %collective-permute-done.31 = f32[64,128]{1,0:T(8,128)S(1)} collective-permute-done((f32[64,128]{1,0:T(8,128)S(1)}, f32[64,128]{1,0:T(8,128)S(1)}, u32[]{:S(2)}, u32[]{:S(2)}) %collective-permute-start.31) | collective-permute-done | bytes 32800 | tf_op jit(solution)/shard_map/ppermute | solution.py:37
  101.6 4.0 %collective-permute-start.36 = (f32[2,64,128]{2,1,0:T(8,128)S(1)}, f32[2,64,128]{2,1,0:T(8,128)S(1)}, u32[]{:S(2)}, u32[]{:S(2)}) collective-permute-start(f32[2,64,128]{2,1,0:T(8,128)S(1)} %pad_maximum_fusion.4), channel_id=1, source_target_pairs={{0,4},{4,0},{1,5},{5,1},{2,6},{6,2},{3,7},{7,3},{8,12},{12,8},{9,1... | collective-permute-start | bytes 196616 | tf_op jit(solution)/shard_map/ppermute | solution.py:37
  105.6 0.6 compare_reduce_fusion
  106.3 0.6 broadcast_in_dim.19
  106.9 8.6 %all-to-all-start = ((f32[64,1,128]{2,1,0:T(1,128)}), f32[64,1,128]{2,1,0:T(1,128)S(1)}, u32[]{:S(2)}, u32[]{:S(2)}) async-start(f32[64,1,128]{2,1,0:T(1,128)} %broadcast_in_dim.19), calls=%async_computation | async-start | bytes 65536 | tf_op jit(solution)/shard_map/all_to_all | solution.py:371
  115.5 8.4 %all-to-all-done = f32[64,1,128]{2,1,0:T(1,128)S(1)} async-done(((f32[64,1,128]{2,1,0:T(1,128)}), f32[64,1,128]{2,1,0:T(1,128)S(1)}, u32[]{:S(2)}, u32[]{:S(2)}) %all-to-all-start) | async-done | bytes 32800 | tf_op jit(solution)/shard_map/all_to_all | solution.py:371
  124.2 2.8 %collective-permute-start.38 = (f32[128,128]{1,0:T(8,128)S(1)}, f32[128,128]{1,0:T(8,128)S(1)}, u32[]{:S(2)}, u32[]{:S(2)}) collective-permute-start(f32[128,128]{1,0:T(8,128)S(1)} %get-tuple-element.42.near0), channel_id=1, source_target_pairs={{0,2},{1,3},{2,0},{3,1},{4,6},{5,7},{6,4},{7,5},{8,10},{9,11},{10,... | collective-permute-start | bytes 196616 | tf_op jit(solution)/shard_map/ppermute | solution.py:37
  126.9 1.9 %collective-permute-start.39 = (f32[128,128]{1,0:T(8,128)S(1)}, f32[128,128]{1,0:T(8,128)S(1)}, u32[]{:S(2)}, u32[]{:S(2)}) collective-permute-start(f32[128,128]{1,0:T(8,128)S(1)} %get-tuple-element.42.near0), channel_id=1, source_target_pairs={{0,3},{1,2},{2,1},{3,0},{4,7},{5,6},{6,5},{7,4},{8,11},{9,10},{10,... | collective-permute-start | bytes 196616 | tf_op jit(solution)/shard_map/ppermute | solution.py:37
  128.8 0.6 broadcast_select_fusion
  129.5 0.9 collective-permute-done.38.near2
  130.4 2.0 %collective-permute-done.39.near3 = f32[128,128]{1,0:T(8,128)S(1)} collective-permute-done((f32[128,128]{1,0:T(8,128)S(1)}, f32[128,128]{1,0:T(8,128)S(1)}, u32[]{:S(2)}, u32[]{:S(2)}) %collective-permute-start.39) | collective-permute-done | bytes 65568 | tf_op jit(solution)/shard_map/ppermute | solution.py:37
  132.5 0.8 shard_map.113
  (76 shorter events, 3.5 us)
Async XLA Ops:
  0.6 20.7 %collective-permute-start = (f32[64,128]{1,0:T(8,128)}, f32[64,128]{1,0:T(8,128)S(1)}, u32[]{:S(2)}, u32[]{:S(2)}) collective-permute-start(f32[64,128]{1,0:T(8,128)} %bitcast.111), channel_id=1, source_target_pairs={{0,64},{8,72},{16,80},{24,88},{32,96},{40,104},{48,112},{56,120},{... | collective-permute-start | bytes 98312 | tf_op jit(solution)/shard_map/ppermute | solution.py:37
  2.6 19.3 %collective-permute-start.1 = (f32[64,128]{1,0:T(8,128)}, f32[64,128]{1,0:T(8,128)S(1)}, u32[]{:S(2)}, u32[]{:S(2)}) collective-permute-start(f32[64,128]{1,0:T(8,128)} %bitcast.112), channel_id=1, source_target_pairs={{0,128},{8,136},{16,144},{24,152},{32,160},{40,168},{48,176},{56,1... | collective-permute-start | bytes 98312 | tf_op jit(solution)/shard_map/ppermute | solution.py:37
  5.9 17.6 %collective-permute-start.2 = (f32[64,128]{1,0:T(8,128)}, f32[64,128]{1,0:T(8,128)S(1)}, u32[]{:S(2)}, u32[]{:S(2)}) collective-permute-start(f32[64,128]{1,0:T(8,128)} %bitcast.113), channel_id=1, source_target_pairs={{0,192},{8,200},{16,208},{24,216},{32,224},{40,232},{48,240},{56,2... | collective-permute-start | bytes 98312 | tf_op jit(solution)/shard_map/ppermute | solution.py:37
  5.9 1.0 copy-start
  7.0 0.7 copy-start.2
  7.6 23.1 %copy-start.1 = (f32[1,1,8,512]{3,2,1,0:T(8,128)S(1)}, f32[1,1,8,512]{3,2,1,0:T(8,128)}, u32[]{:S(2)}) copy-start(f32[1,1,8,512]{3,2,1,0:T(8,128)} %param.10) | copy-start | bytes 49156
  7.9 19.4 %collective-permute-start.4 = (bf16[144,512]{1,0:T(8,128)(2,1)S(1)}, bf16[144,512]{1,0:T(8,128)(2,1)S(1)}, u32[]{:S(2)}, u32[]{:S(2)}) collective-permute-start(bf16[144,512]{1,0:T(8,128)(2,1)S(1)} %get-tuple-element.32), channel_id=1, source_target_pairs={{0,16},{8,24},{16,0},{24,8},{32,48},{40,56},{48,32},{56,40},{64,80... | collective-permute-start | bytes 442376 | tf_op jit(solution)/shard_map/ppermute | solution.py:37
  11.3 7.9 %collective-permute-start.14 = (f32[64,128]{1,0:T(8,128)S(1)}, f32[64,128]{1,0:T(8,128)S(1)}, u32[]{:S(2)}, u32[]{:S(2)}) collective-permute-start(f32[64,128]{1,0:T(8,128)S(1)} %fusion.8), channel_id=1, source_target_pairs={{0,4},{4,0},{1,5},{5,1},{2,6},{6,2},{3,7},{7,3},{8,12},{12,8},{9,1... | collective-permute-start | bytes 98312 | tf_op jit(solution)/shard_map/ppermute | solution.py:37
  19.2 10.1 %collective-permute-start.5 = (bf16[144,512]{1,0:T(8,128)(2,1)S(1)}, bf16[144,512]{1,0:T(8,128)(2,1)S(1)}, u32[]{:S(2)}, u32[]{:S(2)}) collective-permute-start(bf16[144,512]{1,0:T(8,128)(2,1)S(1)} %get-tuple-element.33), channel_id=1, source_target_pairs={{0,32},{8,40},{16,48},{24,56},{32,0},{40,8},{48,16},{56,24},{64,96... | collective-permute-start | bytes 442376 | tf_op jit(solution)/shard_map/ppermute | solution.py:37
  21.3 8.0 %collective-permute-start.6 = (bf16[144,512]{1,0:T(8,128)(2,1)S(1)}, bf16[144,512]{1,0:T(8,128)(2,1)S(1)}, u32[]{:S(2)}, u32[]{:S(2)}) collective-permute-start(bf16[144,512]{1,0:T(8,128)(2,1)S(1)} %get-tuple-element.34), channel_id=1, source_target_pairs={{0,48},{8,56},{16,32},{24,40},{32,16},{40,24},{48,0},{56,8},{64,11... | collective-permute-start | bytes 442376 | tf_op jit(solution)/shard_map/ppermute | solution.py:37
  21.9 5.3 %collective-permute-start.15 = (f32[2,64,128]{2,1,0:T(8,128)S(1)}, f32[2,64,128]{2,1,0:T(8,128)S(1)}, u32[]{:S(2)}, u32[]{:S(2)}) collective-permute-start(f32[2,64,128]{2,1,0:T(8,128)S(1)} %pad_maximum_fusion.2), channel_id=1, source_target_pairs={{0,1},{1,0},{2,3},{3,2},{4,5},{5,4},{6,7},{7,6},{8,9},{9,8},{10,11... | collective-permute-start | bytes 196616 | tf_op jit(solution)/shard_map/ppermute | solution.py:37
  23.5 12.0 %collective-permute-start.16 = (f32[2,64,128]{2,1,0:T(8,128)S(1)}, f32[2,64,128]{2,1,0:T(8,128)S(1)}, u32[]{:S(2)}, u32[]{:S(2)}) collective-permute-start(f32[2,64,128]{2,1,0:T(8,128)S(1)} %pad_maximum_fusion.2), channel_id=1, source_target_pairs={{0,2},{1,3},{2,0},{3,1},{4,6},{5,7},{6,4},{7,5},{8,10},{9,11},{10,... | collective-permute-start | bytes 196616 | tf_op jit(solution)/shard_map/ppermute | solution.py:37
  27.2 2.1 %collective-permute-start.3 = (f32[256,128]{1,0:T(8,128)S(1)}, f32[256,128]{1,0:T(8,128)S(1)}, u32[]{:S(2)}, u32[]{:S(2)}) collective-permute-start(f32[256,128]{1,0:T(8,128)S(1)} %pad_maximum_fusion.own), channel_id=1, source_target_pairs={{0,8},{8,0},{16,24},{24,16},{32,40},{40,32},{48,56},{56,48},{64,72... | collective-permute-start | bytes 393224 | tf_op jit(solution)/shard_map/ppermute | solution.py:37
  27.3 16.3 %collective-permute-start.17 = (f32[2,64,128]{2,1,0:T(8,128)S(1)}, f32[2,64,128]{2,1,0:T(8,128)S(1)}, u32[]{:S(2)}, u32[]{:S(2)}) collective-permute-start(f32[2,64,128]{2,1,0:T(8,128)S(1)} %pad_maximum_fusion.2), channel_id=1, source_target_pairs={{0,3},{1,2},{2,1},{3,0},{4,7},{5,6},{6,5},{7,4},{8,11},{9,10},{10,... | collective-permute-start | bytes 196616 | tf_op jit(solution)/shard_map/ppermute | solution.py:37
  31.6 4.9 %collective-permute-start.7 = (f32[32,512]{1,0:T(8,128)S(1)}, f32[32,512]{1,0:T(8,128)S(1)}, u32[]{:S(2)}, u32[]{:S(2)}) collective-permute-start(f32[32,512]{1,0:T(8,128)S(1)} %shard_map.105.after.part), channel_id=1, source_target_pairs={{0,16},{8,24},{16,0},{24,8},{32,48},{40,56},{48,32},{56,40},{64,80... | collective-permute-start | bytes 196616 | tf_op jit(solution)/shard_map/ppermute | solution.py:37
  33.4 5.8 %collective-permute-start.8 = (f32[32,512]{1,0:T(8,128)S(1)}, f32[32,512]{1,0:T(8,128)S(1)}, u32[]{:S(2)}, u32[]{:S(2)}) collective-permute-start(f32[32,512]{1,0:T(8,128)S(1)} %shard_map.105.after.part), channel_id=1, source_target_pairs={{0,32},{8,40},{16,48},{24,56},{32,0},{40,8},{48,16},{56,24},{64,96... | collective-permute-start | bytes 196616 | tf_op jit(solution)/shard_map/ppermute | solution.py:37
  35.1 5.2 %collective-permute-start.9 = (f32[32,512]{1,0:T(8,128)S(1)}, f32[32,512]{1,0:T(8,128)S(1)}, u32[]{:S(2)}, u32[]{:S(2)}) collective-permute-start(f32[32,512]{1,0:T(8,128)S(1)} %shard_map.105.after.part), channel_id=1, source_target_pairs={{0,48},{8,56},{16,32},{24,40},{32,16},{40,24},{48,0},{56,8},{64,11... | collective-permute-start | bytes 196616 | tf_op jit(solution)/shard_map/ppermute | solution.py:37
  36.5 18.3 %copy-start.3 = (f32[1,8,1024]{2,1,0:T(8,128)S(1)}, f32[1,8,1024]{2,1,0:T(8,128)}, u32[]{:S(2)}) copy-start(f32[1,8,1024]{2,1,0:T(8,128)} %param.14) | copy-start | bytes 98308
  36.5 18.3 %copy-start.4 = (f32[1,8,1024]{2,1,0:T(8,128)S(1)}, f32[1,8,1024]{2,1,0:T(8,128)}, u32[]{:S(2)}) copy-start(f32[1,8,1024]{2,1,0:T(8,128)} %param.13) | copy-start | bytes 98308
  43.3 1.6 %collective-permute-start.10 = (f32[256,128]{1,0:T(8,128)S(1)}, f32[256,128]{1,0:T(8,128)S(1)}, u32[]{:S(2)}, u32[]{:S(2)}) collective-permute-start(f32[256,128]{1,0:T(8,128)S(1)} %get-tuple-element.36), channel_id=1, source_target_pairs={{0,8},{8,0},{16,24},{24,16},{32,40},{40,32},{48,56},{56,48},{64,72... | collective-permute-start | bytes 393224 | tf_op jit(solution)/shard_map/ppermute | solution.py:37
  45.0 4.6 %collective-permute-start.11 = (f32[64,128]{1,0:T(8,128)S(1)}, f32[64,128]{1,0:T(8,128)S(1)}, u32[]{:S(2)}, u32[]{:S(2)}) collective-permute-start(f32[64,128]{1,0:T(8,128)S(1)} %get-tuple-element.58), channel_id=1, source_target_pairs={{0,64},{8,72},{16,80},{24,88},{32,96},{40,104},{48,112},{56,120},{... | collective-permute-start | bytes 98312 | tf_op jit(solution)/shard_map/ppermute | solution.py:37
  45.2 5.8 %collective-permute-start.12 = (f32[64,128]{1,0:T(8,128)S(1)}, f32[64,128]{1,0:T(8,128)S(1)}, u32[]{:S(2)}, u32[]{:S(2)}) collective-permute-start(f32[64,128]{1,0:T(8,128)S(1)} %get-tuple-element.57), channel_id=1, source_target_pairs={{0,128},{8,136},{16,144},{24,152},{32,160},{40,168},{48,176},{56,1... | collective-permute-start | bytes 98312 | tf_op jit(solution)/shard_map/ppermute | solution.py:37
  49.1 5.7 %collective-permute-start.13 = (f32[64,128]{1,0:T(8,128)S(1)}, f32[64,128]{1,0:T(8,128)S(1)}, u32[]{:S(2)}, u32[]{:S(2)}) collective-permute-start(f32[64,128]{1,0:T(8,128)S(1)} %get-tuple-element.56), channel_id=1, source_target_pairs={{0,192},{8,200},{16,208},{24,216},{32,224},{40,232},{48,240},{56,2... | collective-permute-start | bytes 98312 | tf_op jit(solution)/shard_map/ppermute | solution.py:37
  54.9 4.4 %collective-permute-start.18 = (f32[64,128]{1,0:T(8,128)S(1)}, f32[64,128]{1,0:T(8,128)S(1)}, u32[]{:S(2)}, u32[]{:S(2)}) collective-permute-start(f32[64,128]{1,0:T(8,128)S(1)} %fusion.5), channel_id=1, source_target_pairs={{0,64},{8,72},{16,80},{24,88},{32,96},{40,104},{48,112},{56,120},{... | collective-permute-start | bytes 98312 | tf_op jit(solution)/shard_map/ppermute | solution.py:37
  54.9 4.9 %collective-permute-start.19 = (f32[64,128]{1,0:T(8,128)S(1)}, f32[64,128]{1,0:T(8,128)S(1)}, u32[]{:S(2)}, u32[]{:S(2)}) collective-permute-start(f32[64,128]{1,0:T(8,128)S(1)} %fusion.5), channel_id=1, source_target_pairs={{0,128},{8,136},{16,144},{24,152},{32,160},{40,168},{48,176},{56,1... | collective-permute-start | bytes 98312 | tf_op jit(solution)/shard_map/ppermute | solution.py:37
  55.8 5.7 %collective-permute-start.20 = (f32[64,128]{1,0:T(8,128)S(1)}, f32[64,128]{1,0:T(8,128)S(1)}, u32[]{:S(2)}, u32[]{:S(2)}) collective-permute-start(f32[64,128]{1,0:T(8,128)S(1)} %fusion.5), channel_id=1, source_target_pairs={{0,192},{8,200},{16,208},{24,216},{32,224},{40,232},{48,240},{56,2... | collective-permute-start | bytes 98312 | tf_op jit(solution)/shard_map/ppermute | solution.py:37
  61.6 1.4 %collective-permute-start.21 = (f32[256,128]{1,0:T(8,128)S(1)}, f32[256,128]{1,0:T(8,128)S(1)}, u32[]{:S(2)}, u32[]{:S(2)}) collective-permute-start(f32[256,128]{1,0:T(8,128)S(1)} %pad_maximum_fusion.1.own), channel_id=1, source_target_pairs={{0,8},{8,0},{16,24},{24,16},{32,40},{40,32},{48,56},{56,48},{64,72... | collective-permute-start | bytes 393224 | tf_op jit(solution)/shard_map/ppermute | solution.py:37
  63.0 5.8 %collective-permute-start.22 = (f32[8,128]{1,0:T(8,128)S(1)}, f32[8,128]{1,0:T(8,128)S(1)}, u32[]{:S(2)}, u32[]{:S(2)}) collective-permute-start(f32[8,128]{1,0:T(8,128)S(1)} %bitcast_reduce_fusion.refs_2_), channel_id=1, source_target_pairs={{0,16},{8,24},{16,0},{24,8},{32,48},{40,56},{48,32},{56,40},{64,80... | collective-permute-start | bytes 12296 | tf_op jit(solution)/shard_map/ppermute | solution.py:37
  65.9 5.1 %collective-permute-start.23 = (f32[8,128]{1,0:T(8,128)S(1)}, f32[8,128]{1,0:T(8,128)S(1)}, u32[]{:S(2)}, u32[]{:S(2)}) collective-permute-start(f32[8,128]{1,0:T(8,128)S(1)} %bitcast_reduce_fusion.refs_2_), channel_id=1, source_target_pairs={{0,32},{8,40},{16,48},{24,56},{32,0},{40,8},{48,16},{56,24},{64,96... | collective-permute-start | bytes 12296 | tf_op jit(solution)/shard_map/ppermute | solution.py:37
  65.9 5.1 %collective-permute-start.24 = (f32[8,128]{1,0:T(8,128)S(1)}, f32[8,128]{1,0:T(8,128)S(1)}, u32[]{:S(2)}, u32[]{:S(2)}) collective-permute-start(f32[8,128]{1,0:T(8,128)S(1)} %bitcast_reduce_fusion.refs_2_), channel_id=1, source_target_pairs={{0,48},{8,56},{16,32},{24,40},{32,16},{40,24},{48,0},{56,8},{64,11... | collective-permute-start | bytes 12296 | tf_op jit(solution)/shard_map/ppermute | solution.py:37
  73.2 9.7 %collective-permute-start.32 = (f32[64,128]{1,0:T(8,128)S(1)}, f32[64,128]{1,0:T(8,128)S(1)}, u32[]{:S(2)}, u32[]{:S(2)}) collective-permute-start(f32[64,128]{1,0:T(8,128)S(1)} %get-tuple-element.51), channel_id=1, source_target_pairs={{0,4},{4,0},{1,5},{5,1},{2,6},{6,2},{3,7},{7,3},{8,12},{12,8},{9,1... | collective-permute-start | bytes 98312 | tf_op jit(solution)/shard_map/ppermute | solution.py:37
  79.1 7.7 %collective-permute-start.25 = (f32[32,512]{1,0:T(8,128)S(1)}, f32[32,512]{1,0:T(8,128)S(1)}, u32[]{:S(2)}, u32[]{:S(2)}) collective-permute-start(f32[32,512]{1,0:T(8,128)S(1)} %get-tuple-element.37.after.part), channel_id=1, source_target_pairs={{0,16},{8,24},{16,0},{24,8},{32,48},{40,56},{48,32},{56,40},{64,80... | collective-permute-start | bytes 196616 | tf_op jit(solution)/shard_map/ppermute | solution.py:37
  80.7 7.9 %collective-permute-start.26 = (f32[32,512]{1,0:T(8,128)S(1)}, f32[32,512]{1,0:T(8,128)S(1)}, u32[]{:S(2)}, u32[]{:S(2)}) collective-permute-start(f32[32,512]{1,0:T(8,128)S(1)} %get-tuple-element.37.after.part), channel_id=1, source_target_pairs={{0,32},{8,40},{16,48},{24,56},{32,0},{40,8},{48,16},{56,24},{64,96... | collective-permute-start | bytes 196616 | tf_op jit(solution)/shard_map/ppermute | solution.py:37
  82.3 6.4 %collective-permute-start.27 = (f32[32,512]{1,0:T(8,128)S(1)}, f32[32,512]{1,0:T(8,128)S(1)}, u32[]{:S(2)}, u32[]{:S(2)}) collective-permute-start(f32[32,512]{1,0:T(8,128)S(1)} %get-tuple-element.37.after.part), channel_id=1, source_target_pairs={{0,48},{8,56},{16,32},{24,40},{32,16},{40,24},{48,0},{56,8},{64,11... | collective-permute-start | bytes 196616 | tf_op jit(solution)/shard_map/ppermute | solution.py:37
  82.9 8.9 %collective-permute-start.33 = (f32[2,64,128]{2,1,0:T(8,128)S(1)}, f32[2,64,128]{2,1,0:T(8,128)S(1)}, u32[]{:S(2)}, u32[]{:S(2)}) collective-permute-start(f32[2,64,128]{2,1,0:T(8,128)S(1)} %pad_maximum_fusion.3), channel_id=1, source_target_pairs={{0,1},{1,0},{2,3},{3,2},{4,5},{5,4},{6,7},{7,6},{8,9},{9,8},{10,11... | collective-permute-start | bytes 196616 | tf_op jit(solution)/shard_map/ppermute | solution.py:37
  84.0 7.8 %collective-permute-start.34 = (f32[2,64,128]{2,1,0:T(8,128)S(1)}, f32[2,64,128]{2,1,0:T(8,128)S(1)}, u32[]{:S(2)}, u32[]{:S(2)}) collective-permute-start(f32[2,64,128]{2,1,0:T(8,128)S(1)} %pad_maximum_fusion.3), channel_id=1, source_target_pairs={{0,2},{1,3},{2,0},{3,1},{4,6},{5,7},{6,4},{7,5},{8,10},{9,11},{10,... | collective-permute-start | bytes 196616 | tf_op jit(solution)/shard_map/ppermute | solution.py:37
  86.8 5.5 %collective-permute-start.35 = (f32[2,64,128]{2,1,0:T(8,128)S(1)}, f32[2,64,128]{2,1,0:T(8,128)S(1)}, u32[]{:S(2)}, u32[]{:S(2)}) collective-permute-start(f32[2,64,128]{2,1,0:T(8,128)S(1)} %pad_maximum_fusion.3), channel_id=1, source_target_pairs={{0,3},{1,2},{2,1},{3,0},{4,7},{5,6},{6,5},{7,4},{8,11},{9,10},{10,... | collective-permute-start | bytes 196616 | tf_op jit(solution)/shard_map/ppermute | solution.py:37
  91.7 1.4 %collective-permute-start.28 = (f32[256,128]{1,0:T(8,128)S(1)}, f32[256,128]{1,0:T(8,128)S(1)}, u32[]{:S(2)}, u32[]{:S(2)}) collective-permute-start(f32[256,128]{1,0:T(8,128)S(1)} %get-tuple-element.40), channel_id=1, source_target_pairs={{0,8},{8,0},{16,24},{24,16},{32,40},{40,32},{48,56},{56,48},{64,72... | collective-permute-start | bytes 393224 | tf_op jit(solution)/shard_map/ppermute | solution.py:37
  93.2 4.6 %collective-permute-start.29 = (f32[64,128]{1,0:T(8,128)S(1)}, f32[64,128]{1,0:T(8,128)S(1)}, u32[]{:S(2)}, u32[]{:S(2)}) collective-permute-start(f32[64,128]{1,0:T(8,128)S(1)} %get-tuple-element.53), channel_id=1, source_target_pairs={{0,64},{8,72},{16,80},{24,88},{32,96},{40,104},{48,112},{56,120},{... | collective-permute-start | bytes 98312 | tf_op jit(solution)/shard_map/ppermute | solution.py:37
  93.3 5.5 %collective-permute-start.30 = (f32[64,128]{1,0:T(8,128)S(1)}, f32[64,128]{1,0:T(8,128)S(1)}, u32[]{:S(2)}, u32[]{:S(2)}) collective-permute-start(f32[64,128]{1,0:T(8,128)S(1)} %get-tuple-element.55), channel_id=1, source_target_pairs={{0,128},{8,136},{16,144},{24,152},{32,160},{40,168},{48,176},{56,1... | collective-permute-start | bytes 98312 | tf_op jit(solution)/shard_map/ppermute | solution.py:37
  95.8 5.7 %collective-permute-start.31 = (f32[64,128]{1,0:T(8,128)S(1)}, f32[64,128]{1,0:T(8,128)S(1)}, u32[]{:S(2)}, u32[]{:S(2)}) collective-permute-start(f32[64,128]{1,0:T(8,128)S(1)} %get-tuple-element.54), channel_id=1, source_target_pairs={{0,192},{8,200},{16,208},{24,216},{32,224},{40,232},{48,240},{56,2... | collective-permute-start | bytes 98312 | tf_op jit(solution)/shard_map/ppermute | solution.py:37
  101.6 13.9 %collective-permute-start.36 = (f32[2,64,128]{2,1,0:T(8,128)S(1)}, f32[2,64,128]{2,1,0:T(8,128)S(1)}, u32[]{:S(2)}, u32[]{:S(2)}) collective-permute-start(f32[2,64,128]{2,1,0:T(8,128)S(1)} %pad_maximum_fusion.4), channel_id=1, source_target_pairs={{0,4},{4,0},{1,5},{5,1},{2,6},{6,2},{3,7},{7,3},{8,12},{12,8},{9,1... | collective-permute-start | bytes 196616 | tf_op jit(solution)/shard_map/ppermute | solution.py:37
  106.9 17.0 %all-to-all-start = ((f32[64,1,128]{2,1,0:T(1,128)}), f32[64,1,128]{2,1,0:T(1,128)S(1)}, u32[]{:S(2)}, u32[]{:S(2)}) async-start(f32[64,1,128]{2,1,0:T(1,128)} %broadcast_in_dim.19), calls=%async_computation | async-start | bytes 65536 | tf_op jit(solution)/shard_map/all_to_all | solution.py:371
  124.1 5.5 %collective-permute-start.37 = (f32[128,128]{1,0:T(8,128)S(1)}, f32[128,128]{1,0:T(8,128)S(1)}, u32[]{:S(2)}, u32[]{:S(2)}) collective-permute-start(f32[128,128]{1,0:T(8,128)S(1)} %get-tuple-element.42.near0), channel_id=1, source_target_pairs={{0,1},{1,0},{2,3},{3,2},{4,5},{5,4},{6,7},{7,6},{8,9},{9,8},{10,11... | collective-permute-start | bytes 196616 | tf_op jit(solution)/shard_map/ppermute | solution.py:37
  124.2 6.2 %collective-permute-start.38 = (f32[128,128]{1,0:T(8,128)S(1)}, f32[128,128]{1,0:T(8,128)S(1)}, u32[]{:S(2)}, u32[]{:S(2)}) collective-permute-start(f32[128,128]{1,0:T(8,128)S(1)} %get-tuple-element.42.near0), channel_id=1, source_target_pairs={{0,2},{1,3},{2,0},{3,1},{4,6},{5,7},{6,4},{7,5},{8,10},{9,11},{10,... | collective-permute-start | bytes 196616 | tf_op jit(solution)/shard_map/ppermute | solution.py:37
  126.9 5.5 %collective-permute-start.39 = (f32[128,128]{1,0:T(8,128)S(1)}, f32[128,128]{1,0:T(8,128)S(1)}, u32[]{:S(2)}, u32[]{:S(2)}) collective-permute-start(f32[128,128]{1,0:T(8,128)S(1)} %get-tuple-element.42.near0), channel_id=1, source_target_pairs={{0,3},{1,2},{2,1},{3,0},{4,7},{5,6},{6,5},{7,4},{8,11},{9,10},{10,... | collective-permute-start | bytes 196616 | tf_op jit(solution)/shard_map/ppermute | solution.py:37
where the time goes:
time: 134 us; the launch traced here: 133 us
  starting transfers between devices  75.9 us (57%)
  waiting for transfers between devices  32.7 us (24%)
  Pallas kernels  14.6 us (11%)
  other arithmetic  5.19 us (4%)
  local copies, waits for them, and re-layouts  3.78 us (3%)
    ppermute x40, starting transfers between devices, swap(): return lax.ppermute(value, axis, [(i, i ^ mask) for i in range(size)])  67.3 us
    ppermute x40, waiting for transfers between devices, swap(): return lax.ppermute(value, axis, [(i, i ^ mask) for i in range(size)])  24.3 us
    pallas_call x11, Pallas kernels, call(): pl.pallas_call(body, out_shape=[jax.ShapeDtypeStruct(*o) for o in outs],...  14.6 us
    all_to_all x1, starting transfers between devices, body(): lax.all_to_all(jnp.broadcast_to(squares, (64, 1, 128)), ('tm', 'zh'), 0,...  8.57 us
    all_to_all x1, waiting for transfers between devices, body(): lax.all_to_all(jnp.broadcast_to(squares, (64, 1, 128)), ('tm', 'zh'), 0,...  8.44 us
  transfers between devices with their start and end apart: 41, of which 17 were waited for; matrix products, arithmetic and copies ran while one was open for 5% of the time, Pallas kernels for 9%

commit v1 on v0

--- a/solution.py
+++ b/solution.py
@@ -304,8 +304,12 @@
         axis=1,
     )
     rho = jnp.repeat(lax.dynamic_slice_in_dim(rho_dir, tm * 2, 2), 32)[:, None]
-    table = jnp.asarray(poly_basis(channels, degrees))
-    basis = [lax.dynamic_index_in_dim(table, freq ^ d, 0, keepdims=False) for d in range(8)]
+    table = poly_basis(channels, degrees)
+    wide = np.zeros((channels, 8, 128), np.float32)
+    for f in range(channels):
+        wide[f, :, :degrees] = [table[f ^ d] for d in range(8)]
+    rows = lax.dynamic_index_in_dim(jnp.asarray(wide), freq, 0, keepdims=False)
+    basis = [rows[d, :degrees] for d in range(8)]
 
     def y_line(value):
         return [value] + [swap(value, "y", d) for d in (1, 2, 3)]
@@ -367,13 +371,13 @@
     descent = gradient_of(gains, part) + dual_now + rho * (current - fitted)
     near = jnp.stack([current + dual_now / rho, descent])
     far = swap(near, "zh", 1)
-    squares = jnp.sum((descent * descent).reshape(64, 128), axis=0)[None, None, :]
-    squares = lax.all_to_all(jnp.broadcast_to(squares, (64, 1, 128)), ("tm", "zh"), 0, 0, tiled=True).reshape(64, 128)
+    squares = jnp.broadcast_to(jnp.sum(descent * descent, axis=0, keepdims=True), (64, 128))
+    squares = lax.optimization_barrier(squares).reshape(64, 1, 128)
+    squares = lax.all_to_all(squares, ("tm", "zh"), 0, 0, tiled=True).reshape(64, 128)
     args = (zh.astype(jnp.int32).reshape(1), squares, near[0], near[1], far[0], far[1], current)
     outs = [((128, 128), f32), ((64, 128), f32)]
     pair, current = call(functools.partial(step_kernel, count), outs, [], args, smem=1)
     lines = y_line(pair)
-    rows = jnp.zeros((8, 128), f32).at[:, :degrees].set(jnp.stack(basis))
     args = (*lines, rows, current, dual_now, jnp.broadcast_to(rho, (64, 128)))
     outs = [((64, 128), f32), ((64, 128), f32), ((degrees * 64, 128), f32)]
     current, dual_now, poly = call(functools.partial(last_kernel, degrees), outs, [], args)

time: 134 us -> 133 us (level)
  transfers between devices with their start and end apart: 41 -> 41, of which waited for: 17 -> 17; matrix products, arithmetic and copies ran while one was open for 5% -> 4% of each run, Pallas kernels for 9% -> 9%
where the time goes in v1:
time: 133 us
  starting transfers between devices  75.8 us (57%)
  waiting for transfers between devices  33.8 us (25%)
  Pallas kernels  14.6 us (11%)
  other arithmetic  3.91 us (3%)
  local copies, waits for them, and re-layouts  3.43 us (3%)
    ppermute x40, starting transfers between devices, swap(): return lax.ppermute(value, axis, [(i, i ^ mask) for i in range(size)])  67.2 us
    ppermute x40, waiting for transfers between devices, swap(): return lax.ppermute(value, axis, [(i, i ^ mask) for i in range(size)])  25.4 us
    pallas_call x11, Pallas kernels, call(): pl.pallas_call(body, out_shape=[jax.ShapeDtypeStruct(*o) for o in outs],...  14.6 us
    all_to_all x1, starting transfers between devices, body(): lax.all_to_all(squares, ('tm', 'zh'), 0, 0, tiled=True).reshape(64, 128)  8.57 us
    all_to_all x1, waiting for transfers between devices, body(): lax.all_to_all(squares, ('tm', 'zh'), 0, 0, tiled=True).reshape(64, 128)  8.44 us
  transfers between devices with their start and end apart: 41, of which 17 were waited for; matrix products, arithmetic and copies ran while one was open for 4% of the time, Pallas kernels for 9%

profile of v1, /device:TPU:2, one launch (start us, length us, event | category | flops | bytes accessed | tf_op | source)
XLA Modules:
  0.0 132.6 jit_solution(2695053031004202521)
XLA Ops:
  0.6 2.0 %collective-permute-start = (f32[64,128]{1,0:T(8,128)}, f32[64,128]{1,0:T(8,128)S(1)}, u32[]{:S(2)}, u32[]{:S(2)}) collective-permute-start(f32[64,128]{1,0:T(8,128)} %bitcast.114), channel_id=1, source_target_pairs={{0,64},{8,72},{16,80},{24,88},{32,96},{40,104},{48,112},{56,120},{... | collective-permute-start | bytes 98312 | tf_op jit(solution)/shard_map/ppermute | solution.py:37
  2.6 3.3 %collective-permute-start.1 = (f32[64,128]{1,0:T(8,128)}, f32[64,128]{1,0:T(8,128)S(1)}, u32[]{:S(2)}, u32[]{:S(2)}) collective-permute-start(f32[64,128]{1,0:T(8,128)} %bitcast.115), channel_id=1, source_target_pairs={{0,128},{8,136},{16,144},{24,152},{32,160},{40,168},{48,176},{56,1... | collective-permute-start | bytes 98312 | tf_op jit(solution)/shard_map/ppermute | solution.py:37
  5.9 1.0 copy-done
  7.0 0.7 copy-done.2
  7.9 1.5 %collective-permute-start.4 = (bf16[144,512]{1,0:T(8,128)(2,1)S(1)}, bf16[144,512]{1,0:T(8,128)(2,1)S(1)}, u32[]{:S(2)}, u32[]{:S(2)}) collective-permute-start(bf16[144,512]{1,0:T(8,128)(2,1)S(1)} %get-tuple-element.20), channel_id=1, source_target_pairs={{0,16},{8,24},{16,0},{24,8},{32,48},{40,56},{48,32},{56,40},{64,80... | collective-permute-start | bytes 442376 | tf_op jit(solution)/shard_map/ppermute | solution.py:37
  9.4 0.8 select_reduce_fusion
  10.4 0.9 fusion.8
  11.3 5.6 %collective-permute-start.14 = (f32[64,128]{1,0:T(8,128)S(1)}, f32[64,128]{1,0:T(8,128)S(1)}, u32[]{:S(2)}, u32[]{:S(2)}) collective-permute-start(f32[64,128]{1,0:T(8,128)S(1)} %fusion.8), channel_id=1, source_target_pairs={{0,4},{4,0},{1,5},{5,1},{2,6},{6,2},{3,7},{7,3},{8,12},{12,8},{9,1... | collective-permute-start | bytes 98312 | tf_op jit(solution)/shard_map/ppermute | solution.py:37
  16.9 0.9 fusion.6
  17.7 0.7 dynamic-slice_bitcast_fusion.basis
  18.4 0.8 collective-permute-done.14
  19.2 2.0 %collective-permute-start.5 = (bf16[144,512]{1,0:T(8,128)(2,1)S(1)}, bf16[144,512]{1,0:T(8,128)(2,1)S(1)}, u32[]{:S(2)}, u32[]{:S(2)}) collective-permute-start(bf16[144,512]{1,0:T(8,128)(2,1)S(1)} %get-tuple-element.21), channel_id=1, source_target_pairs={{0,32},{8,40},{16,48},{24,56},{32,0},{40,8},{48,16},{56,24},{64,96... | collective-permute-start | bytes 442376 | tf_op jit(solution)/shard_map/ppermute | solution.py:37
  21.2 0.6 collective-permute-start.6
  21.8 1.6 %collective-permute-start.15 = (f32[2,64,128]{2,1,0:T(8,128)S(1)}, f32[2,64,128]{2,1,0:T(8,128)S(1)}, u32[]{:S(2)}, u32[]{:S(2)}) collective-permute-start(f32[2,64,128]{2,1,0:T(8,128)S(1)} %pad_maximum_fusion.2), channel_id=1, source_target_pairs={{0,1},{1,0},{2,3},{3,2},{4,5},{5,4},{6,7},{7,6},{8,9},{9,8},{10,11... | collective-permute-start | bytes 196616 | tf_op jit(solution)/shard_map/ppermute | solution.py:37
  23.4 2.9 %collective-permute-start.16 = (f32[2,64,128]{2,1,0:T(8,128)S(1)}, f32[2,64,128]{2,1,0:T(8,128)S(1)}, u32[]{:S(2)}, u32[]{:S(2)}) collective-permute-start(f32[2,64,128]{2,1,0:T(8,128)S(1)} %pad_maximum_fusion.2), channel_id=1, source_target_pairs={{0,2},{1,3},{2,0},{3,1},{4,6},{5,7},{6,4},{7,5},{8,10},{9,11},{10,... | collective-permute-start | bytes 196616 | tf_op jit(solution)/shard_map/ppermute | solution.py:37
  26.3 0.8 pad_maximum_fusion.own
  27.2 2.0 %collective-permute-start.17 = (f32[2,64,128]{2,1,0:T(8,128)S(1)}, f32[2,64,128]{2,1,0:T(8,128)S(1)}, u32[]{:S(2)}, u32[]{:S(2)}) collective-permute-start(f32[2,64,128]{2,1,0:T(8,128)S(1)} %pad_maximum_fusion.2), channel_id=1, source_target_pairs={{0,3},{1,2},{2,1},{3,0},{4,7},{5,6},{6,5},{7,4},{8,11},{9,10},{10,... | collective-permute-start | bytes 196616 | tf_op jit(solution)/shard_map/ppermute | solution.py:37
  29.2 1.4 %shard_map.104.refs_0_.gains = f32[128,4096]{1,0:T(8,128)S(1)} custom-call(f32[256,128]{1,0:T(8,128)S(1)} %pad_maximum_fusion.own, f32[256,128]{1,0:T(8,128)S(1)} %collective-permute-done.3.other, bf16[144,512]{1,0:T(8,128)(2,1)S(1)} %get-tuple-element.19.sky0.refs_1_.refs_6_, bf16[144,512]{1,0:T(8,128)(2,1)S(1)} %collective-permute-done.4.sky1.refs_2_.refs_7_, ...), custom_call_target="tpu_custom_call" | custom-call | tf_op jit(solution)/shard_map/pallas_call | solution.py:102
  30.6 0.8 shard_map.105.after.part
  31.4 1.8 %collective-permute-start.7 = (f32[32,512]{1,0:T(8,128)S(1)}, f32[32,512]{1,0:T(8,128)S(1)}, u32[]{:S(2)}, u32[]{:S(2)}) collective-permute-start(f32[32,512]{1,0:T(8,128)S(1)} %shard_map.105.after.part), channel_id=1, source_target_pairs={{0,16},{8,24},{16,0},{24,8},{32,48},{40,56},{48,32},{56,40},{64,80... | collective-permute-start | bytes 196616 | tf_op jit(solution)/shard_map/ppermute | solution.py:37
  33.3 1.7 %collective-permute-start.8 = (f32[32,512]{1,0:T(8,128)S(1)}, f32[32,512]{1,0:T(8,128)S(1)}, u32[]{:S(2)}, u32[]{:S(2)}) collective-permute-start(f32[32,512]{1,0:T(8,128)S(1)} %shard_map.105.after.part), channel_id=1, source_target_pairs={{0,32},{8,40},{16,48},{24,56},{32,0},{40,8},{48,16},{56,24},{64,96... | collective-permute-start | bytes 196616 | tf_op jit(solution)/shard_map/ppermute | solution.py:37
  35.0 0.5 collective-permute-start.9
  35.5 0.9 shard_map.106.place
  36.4 2.7 %collective-permute-done.8.r2 = f32[32,512]{1,0:T(8,128)S(1)} collective-permute-done((f32[32,512]{1,0:T(8,128)S(1)}, f32[32,512]{1,0:T(8,128)S(1)}, u32[]{:S(2)}, u32[]{:S(2)}) %collective-permute-start.8) | collective-permute-done | bytes 65568 | tf_op jit(solution)/shard_map/ppermute | solution.py:37
  39.1 1.1 collective-permute-done.9.r3
  40.2 3.0 %shard_map.107 = (f32[256,128]{1,0:T(8,128)S(1)}, f32[256,128]{1,0:T(8,128)S(1)}) custom-call(f32[32,512]{1,0:T(8,128)S(1)} %shard_map.105.after.part, f32[32,512]{1,0:T(8,128)S(1)} %collective-permute-done.7.r1, f32[32,512]{1,0:T(8,128)S(1)} %collective-permute-done.8.r2, f32[32,512]{1,0:T(8,128)S(1)} %collective-permute-done.9.r3, ...), custom_call_target="tpu_custom_call" | custom-call | tf_op jit(solution)/shard_map/pallas_call | solution.py:102
  43.2 0.3 collective-permute-start.10
  43.5 1.3 collective-permute-done.10
  45.1 4.0 %collective-permute-start.12 = (f32[64,128]{1,0:T(8,128)S(1)}, f32[64,128]{1,0:T(8,128)S(1)}, u32[]{:S(2)}, u32[]{:S(2)}) collective-permute-start(f32[64,128]{1,0:T(8,128)S(1)} %get-tuple-element.45), channel_id=1, source_target_pairs={{0,128},{8,136},{16,144},{24,152},{32,160},{40,168},{48,176},{56,1... | collective-permute-start | bytes 98312 | tf_op jit(solution)/shard_map/ppermute | solution.py:37
  49.5 1.9 %collective-permute-done.12 = f32[64,128]{1,0:T(8,128)S(1)} collective-permute-done((f32[64,128]{1,0:T(8,128)S(1)}, f32[64,128]{1,0:T(8,128)S(1)}, u32[]{:S(2)}, u32[]{:S(2)}) %collective-permute-start.12) | collective-permute-done | bytes 32800 | tf_op jit(solution)/shard_map/ppermute | solution.py:37
  51.3 3.5 %collective-permute-done.13 = f32[64,128]{1,0:T(8,128)S(1)} collective-permute-done((f32[64,128]{1,0:T(8,128)S(1)}, f32[64,128]{1,0:T(8,128)S(1)}, u32[]{:S(2)}, u32[]{:S(2)}) %collective-permute-start.13) | collective-permute-done | bytes 32800 | tf_op jit(solution)/shard_map/ppermute | solution.py:37
  54.9 0.9 collective-permute-start.19
  55.8 3.5 %collective-permute-start.20 = (f32[64,128]{1,0:T(8,128)S(1)}, f32[64,128]{1,0:T(8,128)S(1)}, u32[]{:S(2)}, u32[]{:S(2)}) collective-permute-start(f32[64,128]{1,0:T(8,128)S(1)} %fusion.5), channel_id=1, source_target_pairs={{0,192},{8,200},{16,208},{24,216},{32,224},{40,232},{48,240},{56,2... | collective-permute-start | bytes 98312 | tf_op jit(solution)/shard_map/ppermute | solution.py:37
  59.3 0.5 collective-permute-done.19
  59.8 1.7 %collective-permute-done.20 = f32[64,128]{1,0:T(8,128)S(1)} collective-permute-done((f32[64,128]{1,0:T(8,128)S(1)}, f32[64,128]{1,0:T(8,128)S(1)}, u32[]{:S(2)}, u32[]{:S(2)}) %collective-permute-start.20) | collective-permute-done | bytes 32800 | tf_op jit(solution)/shard_map/ppermute | solution.py:37
  61.7 1.3 %collective-permute-done.21.other = f32[256,128]{1,0:T(8,128)S(1)} collective-permute-done((f32[256,128]{1,0:T(8,128)S(1)}, f32[256,128]{1,0:T(8,128)S(1)}, u32[]{:S(2)}, u32[]{:S(2)}) %collective-permute-start.21) | collective-permute-done | bytes 131104 | tf_op jit(solution)/shard_map/ppermute | solution.py:37
  63.0 2.9 %collective-permute-start.22 = (f32[8,128]{1,0:T(8,128)S(1)}, f32[8,128]{1,0:T(8,128)S(1)}, u32[]{:S(2)}, u32[]{:S(2)}) collective-permute-start(f32[8,128]{1,0:T(8,128)S(1)} %bitcast_reduce_fusion.refs_2_), channel_id=1, source_target_pairs={{0,16},{8,24},{16,0},{24,8},{32,48},{40,56},{48,32},{56,40},{64,80... | collective-permute-start | bytes 12296 | tf_op jit(solution)/shard_map/ppermute | solution.py:37
  65.9 1.6 %collective-permute-start.24 = (f32[8,128]{1,0:T(8,128)S(1)}, f32[8,128]{1,0:T(8,128)S(1)}, u32[]{:S(2)}, u32[]{:S(2)}) collective-permute-start(f32[8,128]{1,0:T(8,128)S(1)} %bitcast_reduce_fusion.refs_2_), channel_id=1, source_target_pairs={{0,48},{8,56},{16,32},{24,40},{32,16},{40,24},{48,0},{56,8},{64,11... | collective-permute-start | bytes 12296 | tf_op jit(solution)/shard_map/ppermute | solution.py:37
  67.5 1.4 %shard_map.108.refs_1_ = f32[128,4096]{1,0:T(8,128)S(1)} custom-call(f32[256,128]{1,0:T(8,128)S(1)} %pad_maximum_fusion.1.own, f32[256,128]{1,0:T(8,128)S(1)} %collective-permute-done.21.other, bf16[144,512]{1,0:T(8,128)(2,1)S(1)} %get-tuple-element.19.sky0.refs_1_.refs_6_, bf16[144,512]{1,0:T(8,128)(2,1)S(1)} %collective-permute-done.4.sky1.refs_2_.refs_7_, ...), custom_call_target="tpu_custom_call" | custom-call | tf_op jit(solution)/shard_map/pallas_call | solution.py:102
  68.9 2.2 %collective-permute-done.23.refs_4_ = f32[8,128]{1,0:T(8,128)S(1)} collective-permute-done((f32[8,128]{1,0:T(8,128)S(1)}, f32[8,128]{1,0:T(8,128)S(1)}, u32[]{:S(2)}, u32[]{:S(2)}) %collective-permute-start.23) | collective-permute-done | bytes 4128 | tf_op jit(solution)/shard_map/ppermute | solution.py:37
  71.0 2.0 %shard_map.109 = (f32[128,4096]{1,0:T(8,128)S(1)}, f32[32,512]{1,0:T(8,128)S(1)}, f32[8,128]{1,0:T(8,128)S(1)}) custom-call(f32[128,4096]{1,0:T(8,128)S(1)} %shard_map.104.refs_0_.gains, f32[128,4096]{1,0:T(8,128)S(1)} %shard_map.108.refs_1_, f32[8,128]{1,0:T(8,128)S(1)} %bitcast_reduce_fusion.refs_2_, ...), custom_call_target="tpu_custom_call", output_to_operand_aliasing={{0}: (0, {})} | custom-call | tf_op jit(solution)/shard_map/pallas_call | solution.py:102
  73.2 5.9 %collective-permute-start.32 = (f32[64,128]{1,0:T(8,128)S(1)}, f32[64,128]{1,0:T(8,128)S(1)}, u32[]{:S(2)}, u32[]{:S(2)}) collective-permute-start(f32[64,128]{1,0:T(8,128)S(1)} %get-tuple-element.39), channel_id=1, source_target_pairs={{0,4},{4,0},{1,5},{5,1},{2,6},{6,2},{3,7},{7,3},{8,12},{12,8},{9,1... | collective-permute-start | bytes 98312 | tf_op jit(solution)/shard_map/ppermute | solution.py:37
  79.1 1.6 %collective-permute-start.25 = (f32[32,512]{1,0:T(8,128)S(1)}, f32[32,512]{1,0:T(8,128)S(1)}, u32[]{:S(2)}, u32[]{:S(2)}) collective-permute-start(f32[32,512]{1,0:T(8,128)S(1)} %get-tuple-element.25.after.part), channel_id=1, source_target_pairs={{0,16},{8,24},{16,0},{24,8},{32,48},{40,56},{48,32},{56,40},{64,80... | collective-permute-start | bytes 196616 | tf_op jit(solution)/shard_map/ppermute | solution.py:37
  80.7 1.6 %collective-permute-start.26 = (f32[32,512]{1,0:T(8,128)S(1)}, f32[32,512]{1,0:T(8,128)S(1)}, u32[]{:S(2)}, u32[]{:S(2)}) collective-permute-start(f32[32,512]{1,0:T(8,128)S(1)} %get-tuple-element.25.after.part), channel_id=1, source_target_pairs={{0,32},{8,40},{16,48},{24,56},{32,0},{40,8},{48,16},{56,24},{64,96... | collective-permute-start | bytes 196616 | tf_op jit(solution)/shard_map/ppermute | solution.py:37
  82.3 0.6 collective-permute-start.27
  83.1 0.9 shard_map.110.place
  84.0 2.7 %collective-permute-start.34 = (f32[2,64,128]{2,1,0:T(8,128)S(1)}, f32[2,64,128]{2,1,0:T(8,128)S(1)}, u32[]{:S(2)}, u32[]{:S(2)}) collective-permute-start(f32[2,64,128]{2,1,0:T(8,128)S(1)} %pad_maximum_fusion.3), channel_id=1, source_target_pairs={{0,2},{1,3},{2,0},{3,1},{4,6},{5,7},{6,4},{7,5},{8,10},{9,11},{10,... | collective-permute-start | bytes 196616 | tf_op jit(solution)/shard_map/ppermute | solution.py:37
  86.8 1.9 %collective-permute-start.35 = (f32[2,64,128]{2,1,0:T(8,128)S(1)}, f32[2,64,128]{2,1,0:T(8,128)S(1)}, u32[]{:S(2)}, u32[]{:S(2)}) collective-permute-start(f32[2,64,128]{2,1,0:T(8,128)S(1)} %pad_maximum_fusion.3), channel_id=1, source_target_pairs={{0,3},{1,2},{2,1},{3,0},{4,7},{5,6},{6,5},{7,4},{8,11},{9,10},{10,... | collective-permute-start | bytes 196616 | tf_op jit(solution)/shard_map/ppermute | solution.py:37
  88.7 3.0 %shard_map.111 = (f32[256,128]{1,0:T(8,128)S(1)}, f32[256,128]{1,0:T(8,128)S(1)}) custom-call(f32[32,512]{1,0:T(8,128)S(1)} %get-tuple-element.25.after.part, f32[32,512]{1,0:T(8,128)S(1)} %collective-permute-done.25.r1, f32[32,512]{1,0:T(8,128)S(1)} %collective-permute-done.26.r2, f32[32,512]{1,0:T(8,128)S(1)} %collective-permute-done.27.r3, ...), custom_call_target="tpu_custom_call" | custom-call | tf_op jit(solution)/shard_map/pallas_call | solution.py:102
  91.9 0.4 collective-permute-done.35
  92.4 0.8 collective-permute-done.28
  93.3 2.5 %collective-permute-start.30 = (f32[64,128]{1,0:T(8,128)S(1)}, f32[64,128]{1,0:T(8,128)S(1)}, u32[]{:S(2)}, u32[]{:S(2)}) collective-permute-start(f32[64,128]{1,0:T(8,128)S(1)} %get-tuple-element.43), channel_id=1, source_target_pairs={{0,128},{8,136},{16,144},{24,152},{32,160},{40,168},{48,176},{56,1... | collective-permute-start | bytes 98312 | tf_op jit(solution)/shard_map/ppermute | solution.py:37
  95.8 1.9 %collective-permute-start.31 = (f32[64,128]{1,0:T(8,128)S(1)}, f32[64,128]{1,0:T(8,128)S(1)}, u32[]{:S(2)}, u32[]{:S(2)}) collective-permute-start(f32[64,128]{1,0:T(8,128)S(1)} %get-tuple-element.42), channel_id=1, source_target_pairs={{0,192},{8,200},{16,208},{24,216},{32,224},{40,232},{48,240},{56,2... | collective-permute-start | bytes 98312 | tf_op jit(solution)/shard_map/ppermute | solution.py:37
  97.8 1.0 collective-permute-done.30
  98.8 2.7 %collective-permute-done.31 = f32[64,128]{1,0:T(8,128)S(1)} collective-permute-done((f32[64,128]{1,0:T(8,128)S(1)}, f32[64,128]{1,0:T(8,128)S(1)}, u32[]{:S(2)}, u32[]{:S(2)}) %collective-permute-start.31) | collective-permute-done | bytes 32800 | tf_op jit(solution)/shard_map/ppermute | solution.py:37
  101.6 4.0 %collective-permute-start.36 = (f32[2,64,128]{2,1,0:T(8,128)S(1)}, f32[2,64,128]{2,1,0:T(8,128)S(1)}, u32[]{:S(2)}, u32[]{:S(2)}) collective-permute-start(f32[2,64,128]{2,1,0:T(8,128)S(1)} %pad_maximum_fusion.4), channel_id=1, source_target_pairs={{0,4},{4,0},{1,5},{5,1},{2,6},{6,2},{3,7},{7,3},{8,12},{12,8},{9,1... | collective-permute-start | bytes 196616 | tf_op jit(solution)/shard_map/ppermute | solution.py:37
  105.6 0.6 broadcast_in_dim.30
  106.2 8.6 %all-to-all-start = ((f32[64,1,128]{2,1,0:T(1,128)}), f32[64,1,128]{2,1,0:T(1,128)S(1)}, u32[]{:S(2)}, u32[]{:S(2)}) async-start(f32[64,1,128]{2,1,0:T(1,128)} %bitcast.43), calls=%async_computation | async-start | bytes 65536 | tf_op jit(solution)/shard_map/all_to_all | solution.py:376
  114.8 8.4 %all-to-all-done = f32[64,1,128]{2,1,0:T(1,128)S(1)} async-done(((f32[64,1,128]{2,1,0:T(1,128)}), f32[64,1,128]{2,1,0:T(1,128)S(1)}, u32[]{:S(2)}, u32[]{:S(2)}) %all-to-all-start) | async-done | bytes 32800 | tf_op jit(solution)/shard_map/all_to_all | solution.py:376
  123.5 2.8 %collective-permute-start.38 = (f32[128,128]{1,0:T(8,128)S(1)}, f32[128,128]{1,0:T(8,128)S(1)}, u32[]{:S(2)}, u32[]{:S(2)}) collective-permute-start(f32[128,128]{1,0:T(8,128)S(1)} %get-tuple-element.30.near0), channel_id=1, source_target_pairs={{0,2},{1,3},{2,0},{3,1},{4,6},{5,7},{6,4},{7,5},{8,10},{9,11},{10,... | collective-permute-start | bytes 196616 | tf_op jit(solution)/shard_map/ppermute | solution.py:37
  126.3 1.9 %collective-permute-start.39 = (f32[128,128]{1,0:T(8,128)S(1)}, f32[128,128]{1,0:T(8,128)S(1)}, u32[]{:S(2)}, u32[]{:S(2)}) collective-permute-start(f32[128,128]{1,0:T(8,128)S(1)} %get-tuple-element.30.near0), channel_id=1, source_target_pairs={{0,3},{1,2},{2,1},{3,0},{4,7},{5,6},{6,5},{7,4},{8,11},{9,10},{10,... | collective-permute-start | bytes 196616 | tf_op jit(solution)/shard_map/ppermute | solution.py:37
  128.2 1.5 %collective-permute-done.38.near2 = f32[128,128]{1,0:T(8,128)S(1)} collective-permute-done((f32[128,128]{1,0:T(8,128)S(1)}, f32[128,128]{1,0:T(8,128)S(1)}, u32[]{:S(2)}, u32[]{:S(2)}) %collective-permute-start.38) | collective-permute-done | bytes 65568 | tf_op jit(solution)/shard_map/ppermute | solution.py:37
  129.7 2.0 %collective-permute-done.39.near3 = f32[128,128]{1,0:T(8,128)S(1)} collective-permute-done((f32[128,128]{1,0:T(8,128)S(1)}, f32[128,128]{1,0:T(8,128)S(1)}, u32[]{:S(2)}, u32[]{:S(2)}) %collective-permute-start.39) | collective-permute-done | bytes 65568 | tf_op jit(solution)/shard_map/ppermute | solution.py:37
  131.8 0.8 shard_map.113
  (73 shorter events, 2.7 us)
Async XLA Ops:
  0.6 20.6 %collective-permute-start = (f32[64,128]{1,0:T(8,128)}, f32[64,128]{1,0:T(8,128)S(1)}, u32[]{:S(2)}, u32[]{:S(2)}) collective-permute-start(f32[64,128]{1,0:T(8,128)} %bitcast.114), channel_id=1, source_target_pairs={{0,64},{8,72},{16,80},{24,88},{32,96},{40,104},{48,112},{56,120},{... | collective-permute-start | bytes 98312 | tf_op jit(solution)/shard_map/ppermute | solution.py:37
  2.6 19.2 %collective-permute-start.1 = (f32[64,128]{1,0:T(8,128)}, f32[64,128]{1,0:T(8,128)S(1)}, u32[]{:S(2)}, u32[]{:S(2)}) collective-permute-start(f32[64,128]{1,0:T(8,128)} %bitcast.115), channel_id=1, source_target_pairs={{0,128},{8,136},{16,144},{24,152},{32,160},{40,168},{48,176},{56,1... | collective-permute-start | bytes 98312 | tf_op jit(solution)/shard_map/ppermute | solution.py:37
  5.9 17.5 %collective-permute-start.2 = (f32[64,128]{1,0:T(8,128)}, f32[64,128]{1,0:T(8,128)S(1)}, u32[]{:S(2)}, u32[]{:S(2)}) collective-permute-start(f32[64,128]{1,0:T(8,128)} %bitcast.116), channel_id=1, source_target_pairs={{0,192},{8,200},{16,208},{24,216},{32,224},{40,232},{48,240},{56,2... | collective-permute-start | bytes 98312 | tf_op jit(solution)/shard_map/ppermute | solution.py:37
  5.9 1.0 copy-start
  7.0 0.7 copy-start.2
  7.6 23.0 %copy-start.1 = (f32[1,1,8,512]{3,2,1,0:T(8,128)S(1)}, f32[1,1,8,512]{3,2,1,0:T(8,128)}, u32[]{:S(2)}) copy-start(f32[1,1,8,512]{3,2,1,0:T(8,128)} %param.8) | copy-start | bytes 49156
  7.9 19.3 %collective-permute-start.4 = (bf16[144,512]{1,0:T(8,128)(2,1)S(1)}, bf16[144,512]{1,0:T(8,128)(2,1)S(1)}, u32[]{:S(2)}, u32[]{:S(2)}) collective-permute-start(bf16[144,512]{1,0:T(8,128)(2,1)S(1)} %get-tuple-element.20), channel_id=1, source_target_pairs={{0,16},{8,24},{16,0},{24,8},{32,48},{40,56},{48,32},{56,40},{64,80... | collective-permute-start | bytes 442376 | tf_op jit(solution)/shard_map/ppermute | solution.py:37
  11.3 7.9 %collective-permute-start.14 = (f32[64,128]{1,0:T(8,128)S(1)}, f32[64,128]{1,0:T(8,128)S(1)}, u32[]{:S(2)}, u32[]{:S(2)}) collective-permute-start(f32[64,128]{1,0:T(8,128)S(1)} %fusion.8), channel_id=1, source_target_pairs={{0,4},{4,0},{1,5},{5,1},{2,6},{6,2},{3,7},{7,3},{8,12},{12,8},{9,1... | collective-permute-start | bytes 98312 | tf_op jit(solution)/shard_map/ppermute | solution.py:37
  19.2 10.0 %collective-permute-start.5 = (bf16[144,512]{1,0:T(8,128)(2,1)S(1)}, bf16[144,512]{1,0:T(8,128)(2,1)S(1)}, u32[]{:S(2)}, u32[]{:S(2)}) collective-permute-start(bf16[144,512]{1,0:T(8,128)(2,1)S(1)} %get-tuple-element.21), channel_id=1, source_target_pairs={{0,32},{8,40},{16,48},{24,56},{32,0},{40,8},{48,16},{56,24},{64,96... | collective-permute-start | bytes 442376 | tf_op jit(solution)/shard_map/ppermute | solution.py:37
  21.2 8.0 %collective-permute-start.6 = (bf16[144,512]{1,0:T(8,128)(2,1)S(1)}, bf16[144,512]{1,0:T(8,128)(2,1)S(1)}, u32[]{:S(2)}, u32[]{:S(2)}) collective-permute-start(bf16[144,512]{1,0:T(8,128)(2,1)S(1)} %get-tuple-element.22), channel_id=1, source_target_pairs={{0,48},{8,56},{16,32},{24,40},{32,16},{40,24},{48,0},{56,8},{64,11... | collective-permute-start | bytes 442376 | tf_op jit(solution)/shard_map/ppermute | solution.py:37
  21.8 5.3 %collective-permute-start.15 = (f32[2,64,128]{2,1,0:T(8,128)S(1)}, f32[2,64,128]{2,1,0:T(8,128)S(1)}, u32[]{:S(2)}, u32[]{:S(2)}) collective-permute-start(f32[2,64,128]{2,1,0:T(8,128)S(1)} %pad_maximum_fusion.2), channel_id=1, source_target_pairs={{0,1},{1,0},{2,3},{3,2},{4,5},{5,4},{6,7},{7,6},{8,9},{9,8},{10,11... | collective-permute-start | bytes 196616 | tf_op jit(solution)/shard_map/ppermute | solution.py:37
  23.4 12.0 %collective-permute-start.16 = (f32[2,64,128]{2,1,0:T(8,128)S(1)}, f32[2,64,128]{2,1,0:T(8,128)S(1)}, u32[]{:S(2)}, u32[]{:S(2)}) collective-permute-start(f32[2,64,128]{2,1,0:T(8,128)S(1)} %pad_maximum_fusion.2), channel_id=1, source_target_pairs={{0,2},{1,3},{2,0},{3,1},{4,6},{5,7},{6,4},{7,5},{8,10},{9,11},{10,... | collective-permute-start | bytes 196616 | tf_op jit(solution)/shard_map/ppermute | solution.py:37
  27.1 2.1 %collective-permute-start.3 = (f32[256,128]{1,0:T(8,128)S(1)}, f32[256,128]{1,0:T(8,128)S(1)}, u32[]{:S(2)}, u32[]{:S(2)}) collective-permute-start(f32[256,128]{1,0:T(8,128)S(1)} %pad_maximum_fusion.own), channel_id=1, source_target_pairs={{0,8},{8,0},{16,24},{24,16},{32,40},{40,32},{48,56},{56,48},{64,72... | collective-permute-start | bytes 393224 | tf_op jit(solution)/shard_map/ppermute | solution.py:37
  27.2 16.3 %collective-permute-start.17 = (f32[2,64,128]{2,1,0:T(8,128)S(1)}, f32[2,64,128]{2,1,0:T(8,128)S(1)}, u32[]{:S(2)}, u32[]{:S(2)}) collective-permute-start(f32[2,64,128]{2,1,0:T(8,128)S(1)} %pad_maximum_fusion.2), channel_id=1, source_target_pairs={{0,3},{1,2},{2,1},{3,0},{4,7},{5,6},{6,5},{7,4},{8,11},{9,10},{10,... | collective-permute-start | bytes 196616 | tf_op jit(solution)/shard_map/ppermute | solution.py:37
  31.4 4.9 %collective-permute-start.7 = (f32[32,512]{1,0:T(8,128)S(1)}, f32[32,512]{1,0:T(8,128)S(1)}, u32[]{:S(2)}, u32[]{:S(2)}) collective-permute-start(f32[32,512]{1,0:T(8,128)S(1)} %shard_map.105.after.part), channel_id=1, source_target_pairs={{0,16},{8,24},{16,0},{24,8},{32,48},{40,56},{48,32},{56,40},{64,80... | collective-permute-start | bytes 196616 | tf_op jit(solution)/shard_map/ppermute | solution.py:37
  33.3 5.8 %collective-permute-start.8 = (f32[32,512]{1,0:T(8,128)S(1)}, f32[32,512]{1,0:T(8,128)S(1)}, u32[]{:S(2)}, u32[]{:S(2)}) collective-permute-start(f32[32,512]{1,0:T(8,128)S(1)} %shard_map.105.after.part), channel_id=1, source_target_pairs={{0,32},{8,40},{16,48},{24,56},{32,0},{40,8},{48,16},{56,24},{64,96... | collective-permute-start | bytes 196616 | tf_op jit(solution)/shard_map/ppermute | solution.py:37
  35.0 5.2 %collective-permute-start.9 = (f32[32,512]{1,0:T(8,128)S(1)}, f32[32,512]{1,0:T(8,128)S(1)}, u32[]{:S(2)}, u32[]{:S(2)}) collective-permute-start(f32[32,512]{1,0:T(8,128)S(1)} %shard_map.105.after.part), channel_id=1, source_target_pairs={{0,48},{8,56},{16,32},{24,40},{32,16},{40,24},{48,0},{56,8},{64,11... | collective-permute-start | bytes 196616 | tf_op jit(solution)/shard_map/ppermute | solution.py:37
  36.3 18.5 %copy-start.3 = (f32[1,8,1024]{2,1,0:T(8,128)S(1)}, f32[1,8,1024]{2,1,0:T(8,128)}, u32[]{:S(2)}) copy-start(f32[1,8,1024]{2,1,0:T(8,128)} %param.12) | copy-start | bytes 98308
  36.4 18.4 %copy-start.4 = (f32[1,8,1024]{2,1,0:T(8,128)S(1)}, f32[1,8,1024]{2,1,0:T(8,128)}, u32[]{:S(2)}) copy-start(f32[1,8,1024]{2,1,0:T(8,128)} %param.11) | copy-start | bytes 98308
  43.2 1.6 %collective-permute-start.10 = (f32[256,128]{1,0:T(8,128)S(1)}, f32[256,128]{1,0:T(8,128)S(1)}, u32[]{:S(2)}, u32[]{:S(2)}) collective-permute-start(f32[256,128]{1,0:T(8,128)S(1)} %get-tuple-element.24), channel_id=1, source_target_pairs={{0,8},{8,0},{16,24},{24,16},{32,40},{40,32},{48,56},{56,48},{64,72... | collective-permute-start | bytes 393224 | tf_op jit(solution)/shard_map/ppermute | solution.py:37
  44.9 4.6 %collective-permute-start.11 = (f32[64,128]{1,0:T(8,128)S(1)}, f32[64,128]{1,0:T(8,128)S(1)}, u32[]{:S(2)}, u32[]{:S(2)}) collective-permute-start(f32[64,128]{1,0:T(8,128)S(1)} %get-tuple-element.46), channel_id=1, source_target_pairs={{0,64},{8,72},{16,80},{24,88},{32,96},{40,104},{48,112},{56,120},{... | collective-permute-start | bytes 98312 | tf_op jit(solution)/shard_map/ppermute | solution.py:37
  45.1 6.3 %collective-permute-start.12 = (f32[64,128]{1,0:T(8,128)S(1)}, f32[64,128]{1,0:T(8,128)S(1)}, u32[]{:S(2)}, u32[]{:S(2)}) collective-permute-start(f32[64,128]{1,0:T(8,128)S(1)} %get-tuple-element.45), channel_id=1, source_target_pairs={{0,128},{8,136},{16,144},{24,152},{32,160},{40,168},{48,176},{56,1... | collective-permute-start | bytes 98312 | tf_op jit(solution)/shard_map/ppermute | solution.py:37
  49.1 5.7 %collective-permute-start.13 = (f32[64,128]{1,0:T(8,128)S(1)}, f32[64,128]{1,0:T(8,128)S(1)}, u32[]{:S(2)}, u32[]{:S(2)}) collective-permute-start(f32[64,128]{1,0:T(8,128)S(1)} %get-tuple-element.44), channel_id=1, source_target_pairs={{0,192},{8,200},{16,208},{24,216},{32,224},{40,232},{48,240},{56,2... | collective-permute-start | bytes 98312 | tf_op jit(solution)/shard_map/ppermute | solution.py:37
  54.9 4.4 %collective-permute-start.18 = (f32[64,128]{1,0:T(8,128)S(1)}, f32[64,128]{1,0:T(8,128)S(1)}, u32[]{:S(2)}, u32[]{:S(2)}) collective-permute-start(f32[64,128]{1,0:T(8,128)S(1)} %fusion.5), channel_id=1, source_target_pairs={{0,64},{8,72},{16,80},{24,88},{32,96},{40,104},{48,112},{56,120},{... | collective-permute-start | bytes 98312 | tf_op jit(solution)/shard_map/ppermute | solution.py:37
  54.9 4.9 %collective-permute-start.19 = (f32[64,128]{1,0:T(8,128)S(1)}, f32[64,128]{1,0:T(8,128)S(1)}, u32[]{:S(2)}, u32[]{:S(2)}) collective-permute-start(f32[64,128]{1,0:T(8,128)S(1)} %fusion.5), channel_id=1, source_target_pairs={{0,128},{8,136},{16,144},{24,152},{32,160},{40,168},{48,176},{56,1... | collective-permute-start | bytes 98312 | tf_op jit(solution)/shard_map/ppermute | solution.py:37
  55.8 5.7 %collective-permute-start.20 = (f32[64,128]{1,0:T(8,128)S(1)}, f32[64,128]{1,0:T(8,128)S(1)}, u32[]{:S(2)}, u32[]{:S(2)}) collective-permute-start(f32[64,128]{1,0:T(8,128)S(1)} %fusion.5), channel_id=1, source_target_pairs={{0,192},{8,200},{16,208},{24,216},{32,224},{40,232},{48,240},{56,2... | collective-permute-start | bytes 98312 | tf_op jit(solution)/shard_map/ppermute | solution.py:37
  61.6 1.4 %collective-permute-start.21 = (f32[256,128]{1,0:T(8,128)S(1)}, f32[256,128]{1,0:T(8,128)S(1)}, u32[]{:S(2)}, u32[]{:S(2)}) collective-permute-start(f32[256,128]{1,0:T(8,128)S(1)} %pad_maximum_fusion.1.own), channel_id=1, source_target_pairs={{0,8},{8,0},{16,24},{24,16},{32,40},{40,32},{48,56},{56,48},{64,72... | collective-permute-start | bytes 393224 | tf_op jit(solution)/shard_map/ppermute | solution.py:37
  63.0 5.8 %collective-permute-start.22 = (f32[8,128]{1,0:T(8,128)S(1)}, f32[8,128]{1,0:T(8,128)S(1)}, u32[]{:S(2)}, u32[]{:S(2)}) collective-permute-start(f32[8,128]{1,0:T(8,128)S(1)} %bitcast_reduce_fusion.refs_2_), channel_id=1, source_target_pairs={{0,16},{8,24},{16,0},{24,8},{32,48},{40,56},{48,32},{56,40},{64,80... | collective-permute-start | bytes 12296 | tf_op jit(solution)/shard_map/ppermute | solution.py:37
  65.9 5.1 %collective-permute-start.23 = (f32[8,128]{1,0:T(8,128)S(1)}, f32[8,128]{1,0:T(8,128)S(1)}, u32[]{:S(2)}, u32[]{:S(2)}) collective-permute-start(f32[8,128]{1,0:T(8,128)S(1)} %bitcast_reduce_fusion.refs_2_), channel_id=1, source_target_pairs={{0,32},{8,40},{16,48},{24,56},{32,0},{40,8},{48,16},{56,24},{64,96... | collective-permute-start | bytes 12296 | tf_op jit(solution)/shard_map/ppermute | solution.py:37
  65.9 5.1 %collective-permute-start.24 = (f32[8,128]{1,0:T(8,128)S(1)}, f32[8,128]{1,0:T(8,128)S(1)}, u32[]{:S(2)}, u32[]{:S(2)}) collective-permute-start(f32[8,128]{1,0:T(8,128)S(1)} %bitcast_reduce_fusion.refs_2_), channel_id=1, source_target_pairs={{0,48},{8,56},{16,32},{24,40},{32,16},{40,24},{48,0},{56,8},{64,11... | collective-permute-start | bytes 12296 | tf_op jit(solution)/shard_map/ppermute | solution.py:37
  73.2 9.7 %collective-permute-start.32 = (f32[64,128]{1,0:T(8,128)S(1)}, f32[64,128]{1,0:T(8,128)S(1)}, u32[]{:S(2)}, u32[]{:S(2)}) collective-permute-start(f32[64,128]{1,0:T(8,128)S(1)} %get-tuple-element.39), channel_id=1, source_target_pairs={{0,4},{4,0},{1,5},{5,1},{2,6},{6,2},{3,7},{7,3},{8,12},{12,8},{9,1... | collective-permute-start | bytes 98312 | tf_op jit(solution)/shard_map/ppermute | solution.py:37
  79.1 7.7 %collective-permute-start.25 = (f32[32,512]{1,0:T(8,128)S(1)}, f32[32,512]{1,0:T(8,128)S(1)}, u32[]{:S(2)}, u32[]{:S(2)}) collective-permute-start(f32[32,512]{1,0:T(8,128)S(1)} %get-tuple-element.25.after.part), channel_id=1, source_target_pairs={{0,16},{8,24},{16,0},{24,8},{32,48},{40,56},{48,32},{56,40},{64,80... | collective-permute-start | bytes 196616 | tf_op jit(solution)/shard_map/ppermute | solution.py:37
  80.7 7.9 %collective-permute-start.26 = (f32[32,512]{1,0:T(8,128)S(1)}, f32[32,512]{1,0:T(8,128)S(1)}, u32[]{:S(2)}, u32[]{:S(2)}) collective-permute-start(f32[32,512]{1,0:T(8,128)S(1)} %get-tuple-element.25.after.part), channel_id=1, source_target_pairs={{0,32},{8,40},{16,48},{24,56},{32,0},{40,8},{48,16},{56,24},{64,96... | collective-permute-start | bytes 196616 | tf_op jit(solution)/shard_map/ppermute | solution.py:37
  82.3 6.4 %collective-permute-start.27 = (f32[32,512]{1,0:T(8,128)S(1)}, f32[32,512]{1,0:T(8,128)S(1)}, u32[]{:S(2)}, u32[]{:S(2)}) collective-permute-start(f32[32,512]{1,0:T(8,128)S(1)} %get-tuple-element.25.after.part), channel_id=1, source_target_pairs={{0,48},{8,56},{16,32},{24,40},{32,16},{40,24},{48,0},{56,8},{64,11... | collective-permute-start | bytes 196616 | tf_op jit(solution)/shard_map/ppermute | solution.py:37
  82.9 8.9 %collective-permute-start.33 = (f32[2,64,128]{2,1,0:T(8,128)S(1)}, f32[2,64,128]{2,1,0:T(8,128)S(1)}, u32[]{:S(2)}, u32[]{:S(2)}) collective-permute-start(f32[2,64,128]{2,1,0:T(8,128)S(1)} %pad_maximum_fusion.3), channel_id=1, source_target_pairs={{0,1},{1,0},{2,3},{3,2},{4,5},{5,4},{6,7},{7,6},{8,9},{9,8},{10,11... | collective-permute-start | bytes 196616 | tf_op jit(solution)/shard_map/ppermute | solution.py:37
  84.0 7.8 %collective-permute-start.34 = (f32[2,64,128]{2,1,0:T(8,128)S(1)}, f32[2,64,128]{2,1,0:T(8,128)S(1)}, u32[]{:S(2)}, u32[]{:S(2)}) collective-permute-start(f32[2,64,128]{2,1,0:T(8,128)S(1)} %pad_maximum_fusion.3), channel_id=1, source_target_pairs={{0,2},{1,3},{2,0},{3,1},{4,6},{5,7},{6,4},{7,5},{8,10},{9,11},{10,... | collective-permute-start | bytes 196616 | tf_op jit(solution)/shard_map/ppermute | solution.py:37
  86.8 5.5 %collective-permute-start.35 = (f32[2,64,128]{2,1,0:T(8,128)S(1)}, f32[2,64,128]{2,1,0:T(8,128)S(1)}, u32[]{:S(2)}, u32[]{:S(2)}) collective-permute-start(f32[2,64,128]{2,1,0:T(8,128)S(1)} %pad_maximum_fusion.3), channel_id=1, source_target_pairs={{0,3},{1,2},{2,1},{3,0},{4,7},{5,6},{6,5},{7,4},{8,11},{9,10},{10,... | collective-permute-start | bytes 196616 | tf_op jit(solution)/shard_map/ppermute | solution.py:37
  91.7 1.4 %collective-permute-start.28 = (f32[256,128]{1,0:T(8,128)S(1)}, f32[256,128]{1,0:T(8,128)S(1)}, u32[]{:S(2)}, u32[]{:S(2)}) collective-permute-start(f32[256,128]{1,0:T(8,128)S(1)} %get-tuple-element.28), channel_id=1, source_target_pairs={{0,8},{8,0},{16,24},{24,16},{32,40},{40,32},{48,56},{56,48},{64,72... | collective-permute-start | bytes 393224 | tf_op jit(solution)/shard_map/ppermute | solution.py:37
  93.2 4.6 %collective-permute-start.29 = (f32[64,128]{1,0:T(8,128)S(1)}, f32[64,128]{1,0:T(8,128)S(1)}, u32[]{:S(2)}, u32[]{:S(2)}) collective-permute-start(f32[64,128]{1,0:T(8,128)S(1)} %get-tuple-element.41), channel_id=1, source_target_pairs={{0,64},{8,72},{16,80},{24,88},{32,96},{40,104},{48,112},{56,120},{... | collective-permute-start | bytes 98312 | tf_op jit(solution)/shard_map/ppermute | solution.py:37
  93.3 5.5 %collective-permute-start.30 = (f32[64,128]{1,0:T(8,128)S(1)}, f32[64,128]{1,0:T(8,128)S(1)}, u32[]{:S(2)}, u32[]{:S(2)}) collective-permute-start(f32[64,128]{1,0:T(8,128)S(1)} %get-tuple-element.43), channel_id=1, source_target_pairs={{0,128},{8,136},{16,144},{24,152},{32,160},{40,168},{48,176},{56,1... | collective-permute-start | bytes 98312 | tf_op jit(solution)/shard_map/ppermute | solution.py:37
  95.8 5.7 %collective-permute-start.31 = (f32[64,128]{1,0:T(8,128)S(1)}, f32[64,128]{1,0:T(8,128)S(1)}, u32[]{:S(2)}, u32[]{:S(2)}) collective-permute-start(f32[64,128]{1,0:T(8,128)S(1)} %get-tuple-element.42), channel_id=1, source_target_pairs={{0,192},{8,200},{16,208},{24,216},{32,224},{40,232},{48,240},{56,2... | collective-permute-start | bytes 98312 | tf_op jit(solution)/shard_map/ppermute | solution.py:37
  101.6 13.2 %collective-permute-start.36 = (f32[2,64,128]{2,1,0:T(8,128)S(1)}, f32[2,64,128]{2,1,0:T(8,128)S(1)}, u32[]{:S(2)}, u32[]{:S(2)}) collective-permute-start(f32[2,64,128]{2,1,0:T(8,128)S(1)} %pad_maximum_fusion.4), channel_id=1, source_target_pairs={{0,4},{4,0},{1,5},{5,1},{2,6},{6,2},{3,7},{7,3},{8,12},{12,8},{9,1... | collective-permute-start | bytes 196616 | tf_op jit(solution)/shard_map/ppermute | solution.py:37
  106.2 17.0 %all-to-all-start = ((f32[64,1,128]{2,1,0:T(1,128)}), f32[64,1,128]{2,1,0:T(1,128)S(1)}, u32[]{:S(2)}, u32[]{:S(2)}) async-start(f32[64,1,128]{2,1,0:T(1,128)} %bitcast.43), calls=%async_computation | async-start | bytes 65536 | tf_op jit(solution)/shard_map/all_to_all | solution.py:376
  123.4 4.8 %collective-permute-start.37 = (f32[128,128]{1,0:T(8,128)S(1)}, f32[128,128]{1,0:T(8,128)S(1)}, u32[]{:S(2)}, u32[]{:S(2)}) collective-permute-start(f32[128,128]{1,0:T(8,128)S(1)} %get-tuple-element.30.near0), channel_id=1, source_target_pairs={{0,1},{1,0},{2,3},{3,2},{4,5},{5,4},{6,7},{7,6},{8,9},{9,8},{10,11... | collective-permute-start | bytes 196616 | tf_op jit(solution)/shard_map/ppermute | solution.py:37
  123.5 6.2 %collective-permute-start.38 = (f32[128,128]{1,0:T(8,128)S(1)}, f32[128,128]{1,0:T(8,128)S(1)}, u32[]{:S(2)}, u32[]{:S(2)}) collective-permute-start(f32[128,128]{1,0:T(8,128)S(1)} %get-tuple-element.30.near0), channel_id=1, source_target_pairs={{0,2},{1,3},{2,0},{3,1},{4,6},{5,7},{6,4},{7,5},{8,10},{9,11},{10,... | collective-permute-start | bytes 196616 | tf_op jit(solution)/shard_map/ppermute | solution.py:37
  126.3 5.5 %collective-permute-start.39 = (f32[128,128]{1,0:T(8,128)S(1)}, f32[128,128]{1,0:T(8,128)S(1)}, u32[]{:S(2)}, u32[]{:S(2)}) collective-permute-start(f32[128,128]{1,0:T(8,128)S(1)} %get-tuple-element.30.near0), channel_id=1, source_target_pairs={{0,3},{1,2},{2,1},{3,0},{4,7},{5,6},{6,5},{7,4},{8,11},{9,10},{10,... | collective-permute-start | bytes 196616 | tf_op jit(solution)/shard_map/ppermute | solution.py:37

commit v2 on v1

--- a/solution.py
+++ b/solution.py
@@ -38,7 +38,8 @@
 
 
 def spread(value):
-    own = jnp.concatenate([value] + [swap(value, "tm", 8 * d) for d in (1, 2, 3)], axis=0)
+    parts = [value] + [swap(value, "tm", 8 * d) for d in (1, 2, 3)]
+    own = call(join_kernel, [((256, 128), f32)], [], parts)[0]
     return own, swap(own, "tm", 1)
 
 
@@ -108,6 +109,11 @@
         compiler_params=pltpu.CompilerParams(vmem_limit_bytes=28 << 20),
         input_output_aliases=aliases or {},
     )(*args)
+
+
+def join_kernel(a, b, c, d, out):
+    for i, ref in enumerate((a, b, c, d)):
+        out[i * 64 : i * 64 + 64, :] = ref[...]
 
 
 def last_kernel(degrees, near0, near1, near2, near3, basis, current, dual, rho, out, dual_out, poly):

time: 133 us -> 133 us (level)
  waiting for transfers between devices: 33.8 us -> 35.6 us
  starting transfers between devices: 75.8 us -> 74 us
    ppermute x40, starting transfers between devices: 67.2 us -> 65.4 us  [swap(): return lax.ppermute(value, axis, [(i, i ^ mask) for i in range(size)])]
    ppermute x40, waiting for transfers between devices: 25.4 us -> 27.2 us  [swap(): return lax.ppermute(value, axis, [(i, i ^ mask) for i in range(size)])]
    pallas_call x11 -> x13, Pallas kernels: 14.6 us -> 14.7 us  [call(): pl.pallas_call(body, out_shape=[jax.ShapeDtypeStruct(*o) for o in outs],...]
  transfers between devices with their start and end apart: 41 -> 41, of which waited for: 17 -> 18; matrix products, arithmetic and copies ran while one was open for 4% -> 3% of each run, Pallas kernels for 9% -> 9%
where the time goes in v2:
time: 133 us
  starting transfers between devices  74 us (56%)
  waiting for transfers between devices  35.6 us (27%)
  Pallas kernels  14.7 us (11%)
  local copies, waits for them, and re-layouts  4.19 us (3%)
  other arithmetic  3.14 us (2%)
    ppermute x40, starting transfers between devices, swap(): return lax.ppermute(value, axis, [(i, i ^ mask) for i in range(size)])  65.4 us
    ppermute x40, waiting for transfers between devices, swap(): return lax.ppermute(value, axis, [(i, i ^ mask) for i in range(size)])  27.2 us
    pallas_call x13, Pallas kernels, call(): pl.pallas_call(body, out_shape=[jax.ShapeDtypeStruct(*o) for o in outs],...  14.7 us
    all_to_all x1, starting transfers between devices, body(): lax.all_to_all(squares, ('tm', 'zh'), 0, 0, tiled=True).reshape(64, 128)  8.57 us
    all_to_all x1, waiting for transfers between devices, body(): lax.all_to_all(squares, ('tm', 'zh'), 0, 0, tiled=True).reshape(64, 128)  8.44 us
  transfers between devices with their start and end apart: 41, of which 18 were waited for; matrix products, arithmetic and copies ran while one was open for 3% of the time, Pallas kernels for 9%

profile of v2, /device:TPU:2, one launch (start us, length us, event | category | flops | bytes accessed | tf_op | source)
XLA Modules:
  0.0 132.6 jit_solution(8740356958458448841)
XLA Ops:
  0.6 2.0 %collective-permute-start = (f32[64,128]{1,0:T(8,128)}, f32[64,128]{1,0:T(8,128)S(1)}, u32[]{:S(2)}, u32[]{:S(2)}) collective-permute-start(f32[64,128]{1,0:T(8,128)} %bitcast.107), channel_id=1, source_target_pairs={{0,64},{8,72},{16,80},{24,88},{32,96},{40,104},{48,112},{56,120},{... | collective-permute-start | bytes 98312 | tf_op jit(solution)/shard_map/ppermute | solution.py:37
  2.6 3.3 %collective-permute-start.1 = (f32[64,128]{1,0:T(8,128)}, f32[64,128]{1,0:T(8,128)S(1)}, u32[]{:S(2)}, u32[]{:S(2)}) collective-permute-start(f32[64,128]{1,0:T(8,128)} %bitcast.108), channel_id=1, source_target_pairs={{0,128},{8,136},{16,144},{24,152},{32,160},{40,168},{48,176},{56,1... | collective-permute-start | bytes 98312 | tf_op jit(solution)/shard_map/ppermute | solution.py:37
  5.9 1.0 copy-done.2
  7.0 0.7 copy-done.4
  7.9 1.5 %collective-permute-start.4 = (bf16[144,512]{1,0:T(8,128)(2,1)S(1)}, bf16[144,512]{1,0:T(8,128)(2,1)S(1)}, u32[]{:S(2)}, u32[]{:S(2)}) collective-permute-start(bf16[144,512]{1,0:T(8,128)(2,1)S(1)} %get-tuple-element.20), channel_id=1, source_target_pairs={{0,16},{8,24},{16,0},{24,8},{32,48},{40,56},{48,32},{56,40},{64,80... | collective-permute-start | bytes 442376 | tf_op jit(solution)/shard_map/ppermute | solution.py:37
  9.4 0.8 select_reduce_fusion
  10.4 0.9 fusion.8
  11.3 5.6 %collective-permute-start.14 = (f32[64,128]{1,0:T(8,128)S(1)}, f32[64,128]{1,0:T(8,128)S(1)}, u32[]{:S(2)}, u32[]{:S(2)}) collective-permute-start(f32[64,128]{1,0:T(8,128)S(1)} %fusion.8), channel_id=1, source_target_pairs={{0,4},{4,0},{1,5},{5,1},{2,6},{6,2},{3,7},{7,3},{8,12},{12,8},{9,1... | collective-permute-start | bytes 98312 | tf_op jit(solution)/shard_map/ppermute | solution.py:37
  16.9 0.9 fusion.6
  17.7 0.7 dynamic-slice_bitcast_fusion.basis
  18.4 0.8 collective-permute-done.14
  19.2 1.1 collective-permute-start.15
  20.4 2.5 %collective-permute-start.5 = (bf16[144,512]{1,0:T(8,128)(2,1)S(1)}, bf16[144,512]{1,0:T(8,128)(2,1)S(1)}, u32[]{:S(2)}, u32[]{:S(2)}) collective-permute-start(bf16[144,512]{1,0:T(8,128)(2,1)S(1)} %get-tuple-element.21), channel_id=1, source_target_pairs={{0,32},{8,40},{16,48},{24,56},{32,0},{40,8},{48,16},{56,24},{64,96... | collective-permute-start | bytes 442376 | tf_op jit(solution)/shard_map/ppermute | solution.py:37
  22.9 0.5 collective-permute-start.6
  23.4 2.9 %collective-permute-start.16 = (f32[2,64,128]{2,1,0:T(8,128)S(1)}, f32[2,64,128]{2,1,0:T(8,128)S(1)}, u32[]{:S(2)}, u32[]{:S(2)}) collective-permute-start(f32[2,64,128]{2,1,0:T(8,128)S(1)} %pad_maximum_fusion), channel_id=1, source_target_pairs={{0,2},{1,3},{2,0},{3,1},{4,6},{5,7},{6,4},{7,5},{8,10},{9,11},{10,... | collective-permute-start | bytes 196616 | tf_op jit(solution)/shard_map/ppermute | solution.py:37
  26.3 0.8 copy-done
  27.2 0.3 collective-permute-start.17
  27.5 1.3 collective-permute-done.6.sky3.refs_4_.refs_9_
  28.8 1.4 %shard_map.105.refs_0_.gains = f32[128,4096]{1,0:T(8,128)S(1)} custom-call(f32[256,128]{1,0:T(8,128)S(1)} %shard_map.103.own, f32[256,128]{1,0:T(8,128)S(1)} %collective-permute-done.3.other, bf16[144,512]{1,0:T(8,128)(2,1)S(1)} %get-tuple-element.19.sky0.refs_1_.refs_6_, bf16[144,512]{1,0:T(8,128)(2,1)S(1)} %collective-permute-done.4.sky1.refs_2_.refs_7_, ...), custom_call_target="tpu_custom_call" | custom-call | tf_op jit(solution)/shard_map/pallas_call | solution.py:103
  30.2 0.8 shard_map.106.after.part
  31.0 2.3 %collective-permute-start.7 = (f32[32,512]{1,0:T(8,128)S(1)}, f32[32,512]{1,0:T(8,128)S(1)}, u32[]{:S(2)}, u32[]{:S(2)}) collective-permute-start(f32[32,512]{1,0:T(8,128)S(1)} %shard_map.106.after.part), channel_id=1, source_target_pairs={{0,16},{8,24},{16,0},{24,8},{32,48},{40,56},{48,32},{56,40},{64,80... | collective-permute-start | bytes 196616 | tf_op jit(solution)/shard_map/ppermute | solution.py:37
  33.3 0.9 collective-permute-start.8
  34.3 0.6 collective-permute-start.9
  34.9 0.9 shard_map.107.place
  35.8 3.4 %collective-permute-done.8.r2 = f32[32,512]{1,0:T(8,128)S(1)} collective-permute-done((f32[32,512]{1,0:T(8,128)S(1)}, f32[32,512]{1,0:T(8,128)S(1)}, u32[]{:S(2)}, u32[]{:S(2)}) %collective-permute-start.8) | collective-permute-done | bytes 65568 | tf_op jit(solution)/shard_map/ppermute | solution.py:37
  39.4 3.0 %shard_map.108 = (f32[256,128]{1,0:T(8,128)S(1)}, f32[256,128]{1,0:T(8,128)S(1)}) custom-call(f32[32,512]{1,0:T(8,128)S(1)} %shard_map.106.after.part, f32[32,512]{1,0:T(8,128)S(1)} %collective-permute-done.7.r1, f32[32,512]{1,0:T(8,128)S(1)} %collective-permute-done.8.r2, f32[32,512]{1,0:T(8,128)S(1)} %collective-permute-done.9.r3, ...), custom_call_target="tpu_custom_call" | custom-call | tf_op jit(solution)/shard_map/pallas_call | solution.py:103
  42.4 0.3 collective-permute-start.10
  42.7 1.3 collective-permute-done.10
  44.3 4.0 %collective-permute-start.12 = (f32[64,128]{1,0:T(8,128)S(1)}, f32[64,128]{1,0:T(8,128)S(1)}, u32[]{:S(2)}, u32[]{:S(2)}) collective-permute-start(f32[64,128]{1,0:T(8,128)S(1)} %get-tuple-element.45), channel_id=1, source_target_pairs={{0,128},{8,136},{16,144},{24,152},{32,160},{40,168},{48,176},{56,1... | collective-permute-start | bytes 98312 | tf_op jit(solution)/shard_map/ppermute | solution.py:37
  48.7 1.5 %collective-permute-done.12 = f32[64,128]{1,0:T(8,128)S(1)} collective-permute-done((f32[64,128]{1,0:T(8,128)S(1)}, f32[64,128]{1,0:T(8,128)S(1)}, u32[]{:S(2)}, u32[]{:S(2)}) %collective-permute-start.12) | collective-permute-done | bytes 32800 | tf_op jit(solution)/shard_map/ppermute | solution.py:37
  50.2 3.8 %collective-permute-done.13 = f32[64,128]{1,0:T(8,128)S(1)} collective-permute-done((f32[64,128]{1,0:T(8,128)S(1)}, f32[64,128]{1,0:T(8,128)S(1)}, u32[]{:S(2)}, u32[]{:S(2)}) %collective-permute-start.13) | collective-permute-done | bytes 32800 | tf_op jit(solution)/shard_map/ppermute | solution.py:37
  54.1 0.9 collective-permute-start.19
  55.1 3.5 %collective-permute-start.20 = (f32[64,128]{1,0:T(8,128)S(1)}, f32[64,128]{1,0:T(8,128)S(1)}, u32[]{:S(2)}, u32[]{:S(2)}) collective-permute-start(f32[64,128]{1,0:T(8,128)S(1)} %fusion.5.a), channel_id=1, source_target_pairs={{0,192},{8,200},{16,208},{24,216},{32,224},{40,232},{48,240},{56,2... | collective-permute-start | bytes 98312 | tf_op jit(solution)/shard_map/ppermute | solution.py:37
  58.5 0.5 collective-permute-done.19.c
  59.0 1.7 %collective-permute-done.20.d = f32[64,128]{1,0:T(8,128)S(1)} collective-permute-done((f32[64,128]{1,0:T(8,128)S(1)}, f32[64,128]{1,0:T(8,128)S(1)}, u32[]{:S(2)}, u32[]{:S(2)}) %collective-permute-start.20) | collective-permute-done | bytes 32800 | tf_op jit(solution)/shard_map/ppermute | solution.py:37
  60.9 1.3 %collective-permute-done.21.other = f32[256,128]{1,0:T(8,128)S(1)} collective-permute-done((f32[256,128]{1,0:T(8,128)S(1)}, f32[256,128]{1,0:T(8,128)S(1)}, u32[]{:S(2)}, u32[]{:S(2)}) %collective-permute-start.21) | collective-permute-done | bytes 131104 | tf_op jit(solution)/shard_map/ppermute | solution.py:37
  62.3 3.0 %collective-permute-start.22 = (f32[8,128]{1,0:T(8,128)S(1)}, f32[8,128]{1,0:T(8,128)S(1)}, u32[]{:S(2)}, u32[]{:S(2)}) collective-permute-start(f32[8,128]{1,0:T(8,128)S(1)} %bitcast_reduce_fusion.refs_2_), channel_id=1, source_target_pairs={{0,16},{8,24},{16,0},{24,8},{32,48},{40,56},{48,32},{56,40},{64,80... | collective-permute-start | bytes 12296 | tf_op jit(solution)/shard_map/ppermute | solution.py:37
  65.4 1.4 %collective-permute-start.24 = (f32[8,128]{1,0:T(8,128)S(1)}, f32[8,128]{1,0:T(8,128)S(1)}, u32[]{:S(2)}, u32[]{:S(2)}) collective-permute-start(f32[8,128]{1,0:T(8,128)S(1)} %bitcast_reduce_fusion.refs_2_), channel_id=1, source_target_pairs={{0,48},{8,56},{16,32},{24,40},{32,16},{40,24},{48,0},{56,8},{64,11... | collective-permute-start | bytes 12296 | tf_op jit(solution)/shard_map/ppermute | solution.py:37
  66.8 1.4 %shard_map.110.refs_1_ = f32[128,4096]{1,0:T(8,128)S(1)} custom-call(f32[256,128]{1,0:T(8,128)S(1)} %shard_map.109.own, f32[256,128]{1,0:T(8,128)S(1)} %collective-permute-done.21.other, bf16[144,512]{1,0:T(8,128)(2,1)S(1)} %get-tuple-element.19.sky0.refs_1_.refs_6_, bf16[144,512]{1,0:T(8,128)(2,1)S(1)} %collective-permute-done.4.sky1.refs_2_.refs_7_, ...), custom_call_target="tpu_custom_call" | custom-call | tf_op jit(solution)/shard_map/pallas_call | solution.py:103
  68.2 2.2 %collective-permute-done.23.refs_4_ = f32[8,128]{1,0:T(8,128)S(1)} collective-permute-done((f32[8,128]{1,0:T(8,128)S(1)}, f32[8,128]{1,0:T(8,128)S(1)}, u32[]{:S(2)}, u32[]{:S(2)}) %collective-permute-start.23) | collective-permute-done | bytes 4128 | tf_op jit(solution)/shard_map/ppermute | solution.py:37
  70.3 2.0 %shard_map.111 = (f32[128,4096]{1,0:T(8,128)S(1)}, f32[32,512]{1,0:T(8,128)S(1)}, f32[8,128]{1,0:T(8,128)S(1)}) custom-call(f32[128,4096]{1,0:T(8,128)S(1)} %shard_map.105.refs_0_.gains, f32[128,4096]{1,0:T(8,128)S(1)} %shard_map.110.refs_1_, f32[8,128]{1,0:T(8,128)S(1)} %bitcast_reduce_fusion.refs_2_, ...), custom_call_target="tpu_custom_call", output_to_operand_aliasing={{0}: (0, {})} | custom-call | tf_op jit(solution)/shard_map/pallas_call | solution.py:103
  72.5 5.9 %collective-permute-start.32 = (f32[64,128]{1,0:T(8,128)S(1)}, f32[64,128]{1,0:T(8,128)S(1)}, u32[]{:S(2)}, u32[]{:S(2)}) collective-permute-start(f32[64,128]{1,0:T(8,128)S(1)} %get-tuple-element.39), channel_id=1, source_target_pairs={{0,4},{4,0},{1,5},{5,1},{2,6},{6,2},{3,7},{7,3},{8,12},{12,8},{9,1... | collective-permute-start | bytes 98312 | tf_op jit(solution)/shard_map/ppermute | solution.py:37
  78.4 2.4 %collective-permute-start.25 = (f32[32,512]{1,0:T(8,128)S(1)}, f32[32,512]{1,0:T(8,128)S(1)}, u32[]{:S(2)}, u32[]{:S(2)}) collective-permute-start(f32[32,512]{1,0:T(8,128)S(1)} %get-tuple-element.25.after.part), channel_id=1, source_target_pairs={{0,16},{8,24},{16,0},{24,8},{32,48},{40,56},{48,32},{56,40},{64,80... | collective-permute-start | bytes 196616 | tf_op jit(solution)/shard_map/ppermute | solution.py:37
  80.8 0.8 collective-permute-start.26
  81.6 0.6 collective-permute-start.27
  82.3 0.6 collective-permute-start.33
  82.8 0.9 shard_map.112.place
  83.7 3.3 %collective-permute-start.34 = (f32[2,64,128]{2,1,0:T(8,128)S(1)}, f32[2,64,128]{2,1,0:T(8,128)S(1)}, u32[]{:S(2)}, u32[]{:S(2)}) collective-permute-start(f32[2,64,128]{2,1,0:T(8,128)S(1)} %pad_maximum_fusion.1), channel_id=1, source_target_pairs={{0,2},{1,3},{2,0},{3,1},{4,6},{5,7},{6,4},{7,5},{8,10},{9,11},{10,... | collective-permute-start | bytes 196616 | tf_op jit(solution)/shard_map/ppermute | solution.py:37
  87.0 1.0 collective-permute-start.35
  88.0 3.0 %shard_map.113 = (f32[256,128]{1,0:T(8,128)S(1)}, f32[256,128]{1,0:T(8,128)S(1)}) custom-call(f32[32,512]{1,0:T(8,128)S(1)} %get-tuple-element.25.after.part, f32[32,512]{1,0:T(8,128)S(1)} %collective-permute-done.25.r1, f32[32,512]{1,0:T(8,128)S(1)} %collective-permute-done.26.r2, f32[32,512]{1,0:T(8,128)S(1)} %collective-permute-done.27.r3, ...), custom_call_target="tpu_custom_call" | custom-call | tf_op jit(solution)/shard_map/pallas_call | solution.py:103
  91.2 1.2 collective-permute-done.35
  92.8 2.5 %collective-permute-start.30 = (f32[64,128]{1,0:T(8,128)S(1)}, f32[64,128]{1,0:T(8,128)S(1)}, u32[]{:S(2)}, u32[]{:S(2)}) collective-permute-start(f32[64,128]{1,0:T(8,128)S(1)} %get-tuple-element.43), channel_id=1, source_target_pairs={{0,128},{8,136},{16,144},{24,152},{32,160},{40,168},{48,176},{56,1... | collective-permute-start | bytes 98312 | tf_op jit(solution)/shard_map/ppermute | solution.py:37
  95.2 1.9 %collective-permute-start.31 = (f32[64,128]{1,0:T(8,128)S(1)}, f32[64,128]{1,0:T(8,128)S(1)}, u32[]{:S(2)}, u32[]{:S(2)}) collective-permute-start(f32[64,128]{1,0:T(8,128)S(1)} %get-tuple-element.42), channel_id=1, source_target_pairs={{0,192},{8,200},{16,208},{24,216},{32,224},{40,232},{48,240},{56,2... | collective-permute-start | bytes 98312 | tf_op jit(solution)/shard_map/ppermute | solution.py:37
  97.2 1.0 collective-permute-done.30
  98.2 2.7 %collective-permute-done.31 = f32[64,128]{1,0:T(8,128)S(1)} collective-permute-done((f32[64,128]{1,0:T(8,128)S(1)}, f32[64,128]{1,0:T(8,128)S(1)}, u32[]{:S(2)}, u32[]{:S(2)}) %collective-permute-start.31) | collective-permute-done | bytes 32800 | tf_op jit(solution)/shard_map/ppermute | solution.py:37
  101.0 3.9 %collective-permute-start.36 = (f32[2,64,128]{2,1,0:T(8,128)S(1)}, f32[2,64,128]{2,1,0:T(8,128)S(1)}, u32[]{:S(2)}, u32[]{:S(2)}) collective-permute-start(f32[2,64,128]{2,1,0:T(8,128)S(1)} %pad_maximum_fusion.2), channel_id=1, source_target_pairs={{0,4},{4,0},{1,5},{5,1},{2,6},{6,2},{3,7},{7,3},{8,12},{12,8},{9,1... | collective-permute-start | bytes 196616 | tf_op jit(solution)/shard_map/ppermute | solution.py:37
  104.9 0.6 broadcast_in_dim.30
  105.5 8.6 %all-to-all-start = ((f32[64,1,128]{2,1,0:T(1,128)}), f32[64,1,128]{2,1,0:T(1,128)S(1)}, u32[]{:S(2)}, u32[]{:S(2)}) async-start(f32[64,1,128]{2,1,0:T(1,128)} %bitcast.43), calls=%async_computation | async-start | bytes 65536 | tf_op jit(solution)/shard_map/all_to_all | solution.py:382
  114.1 8.4 %all-to-all-done = f32[64,1,128]{2,1,0:T(1,128)S(1)} async-done(((f32[64,1,128]{2,1,0:T(1,128)}), f32[64,1,128]{2,1,0:T(1,128)S(1)}, u32[]{:S(2)}, u32[]{:S(2)}) %all-to-all-start) | async-done | bytes 32800 | tf_op jit(solution)/shard_map/all_to_all | solution.py:382
  122.8 3.5 %collective-permute-start.38 = (f32[128,128]{1,0:T(8,128)S(1)}, f32[128,128]{1,0:T(8,128)S(1)}, u32[]{:S(2)}, u32[]{:S(2)}) collective-permute-start(f32[128,128]{1,0:T(8,128)S(1)} %get-tuple-element.30.near0), channel_id=1, source_target_pairs={{0,2},{1,3},{2,0},{3,1},{4,6},{5,7},{6,4},{7,5},{8,10},{9,11},{10,... | collective-permute-start | bytes 196616 | tf_op jit(solution)/shard_map/ppermute | solution.py:37
  126.3 1.2 collective-permute-start.39
  127.6 1.9 %collective-permute-done.38.near2 = f32[128,128]{1,0:T(8,128)S(1)} collective-permute-done((f32[128,128]{1,0:T(8,128)S(1)}, f32[128,128]{1,0:T(8,128)S(1)}, u32[]{:S(2)}, u32[]{:S(2)}) %collective-permute-start.38) | collective-permute-done | bytes 65568 | tf_op jit(solution)/shard_map/ppermute | solution.py:37
  129.6 2.2 %collective-permute-done.39.near3 = f32[128,128]{1,0:T(8,128)S(1)} collective-permute-done((f32[128,128]{1,0:T(8,128)S(1)}, f32[128,128]{1,0:T(8,128)S(1)}, u32[]{:S(2)}, u32[]{:S(2)}) %collective-permute-start.39) | collective-permute-done | bytes 65568 | tf_op jit(solution)/shard_map/ppermute | solution.py:37
  131.8 0.8 shard_map.115
  (75 shorter events, 3.0 us)
Async XLA Ops:
  0.6 19.7 %collective-permute-start = (f32[64,128]{1,0:T(8,128)}, f32[64,128]{1,0:T(8,128)S(1)}, u32[]{:S(2)}, u32[]{:S(2)}) collective-permute-start(f32[64,128]{1,0:T(8,128)} %bitcast.107), channel_id=1, source_target_pairs={{0,64},{8,72},{16,80},{24,88},{32,96},{40,104},{48,112},{56,120},{... | collective-permute-start | bytes 98312 | tf_op jit(solution)/shard_map/ppermute | solution.py:37
  2.6 20.2 %collective-permute-start.1 = (f32[64,128]{1,0:T(8,128)}, f32[64,128]{1,0:T(8,128)S(1)}, u32[]{:S(2)}, u32[]{:S(2)}) collective-permute-start(f32[64,128]{1,0:T(8,128)} %bitcast.108), channel_id=1, source_target_pairs={{0,128},{8,136},{16,144},{24,152},{32,160},{40,168},{48,176},{56,1... | collective-permute-start | bytes 98312 | tf_op jit(solution)/shard_map/ppermute | solution.py:37
  5.9 17.5 %collective-permute-start.2 = (f32[64,128]{1,0:T(8,128)}, f32[64,128]{1,0:T(8,128)S(1)}, u32[]{:S(2)}, u32[]{:S(2)}) collective-permute-start(f32[64,128]{1,0:T(8,128)} %bitcast.109), channel_id=1, source_target_pairs={{0,192},{8,200},{16,208},{24,216},{32,224},{40,232},{48,240},{56,2... | collective-permute-start | bytes 98312 | tf_op jit(solution)/shard_map/ppermute | solution.py:37
  5.9 1.0 copy-start.2
  7.0 0.7 copy-start.4
  7.6 22.5 %copy-start.3 = (f32[1,1,8,512]{3,2,1,0:T(8,128)S(1)}, f32[1,1,8,512]{3,2,1,0:T(8,128)}, u32[]{:S(2)}) copy-start(f32[1,1,8,512]{3,2,1,0:T(8,128)} %param.8) | copy-start | bytes 49156
  7.9 19.3 %collective-permute-start.4 = (bf16[144,512]{1,0:T(8,128)(2,1)S(1)}, bf16[144,512]{1,0:T(8,128)(2,1)S(1)}, u32[]{:S(2)}, u32[]{:S(2)}) collective-permute-start(bf16[144,512]{1,0:T(8,128)(2,1)S(1)} %get-tuple-element.20), channel_id=1, source_target_pairs={{0,16},{8,24},{16,0},{24,8},{32,48},{40,56},{48,32},{56,40},{64,80... | collective-permute-start | bytes 442376 | tf_op jit(solution)/shard_map/ppermute | solution.py:37
  11.3 7.9 %collective-permute-start.14 = (f32[64,128]{1,0:T(8,128)S(1)}, f32[64,128]{1,0:T(8,128)S(1)}, u32[]{:S(2)}, u32[]{:S(2)}) collective-permute-start(f32[64,128]{1,0:T(8,128)S(1)} %fusion.8), channel_id=1, source_target_pairs={{0,4},{4,0},{1,5},{5,1},{2,6},{6,2},{3,7},{7,3},{8,12},{12,8},{9,1... | collective-permute-start | bytes 98312 | tf_op jit(solution)/shard_map/ppermute | solution.py:37
  19.2 7.9 %collective-permute-start.15 = (f32[2,64,128]{2,1,0:T(8,128)S(1)}, f32[2,64,128]{2,1,0:T(8,128)S(1)}, u32[]{:S(2)}, u32[]{:S(2)}) collective-permute-start(f32[2,64,128]{2,1,0:T(8,128)S(1)} %pad_maximum_fusion), channel_id=1, source_target_pairs={{0,1},{1,0},{2,3},{3,2},{4,5},{5,4},{6,7},{7,6},{8,9},{9,8},{10,11... | collective-permute-start | bytes 196616 | tf_op jit(solution)/shard_map/ppermute | solution.py:37
  20.4 7.2 %collective-permute-start.5 = (bf16[144,512]{1,0:T(8,128)(2,1)S(1)}, bf16[144,512]{1,0:T(8,128)(2,1)S(1)}, u32[]{:S(2)}, u32[]{:S(2)}) collective-permute-start(bf16[144,512]{1,0:T(8,128)(2,1)S(1)} %get-tuple-element.21), channel_id=1, source_target_pairs={{0,32},{8,40},{16,48},{24,56},{32,0},{40,8},{48,16},{56,24},{64,96... | collective-permute-start | bytes 442376 | tf_op jit(solution)/shard_map/ppermute | solution.py:37
  22.9 5.9 %collective-permute-start.6 = (bf16[144,512]{1,0:T(8,128)(2,1)S(1)}, bf16[144,512]{1,0:T(8,128)(2,1)S(1)}, u32[]{:S(2)}, u32[]{:S(2)}) collective-permute-start(bf16[144,512]{1,0:T(8,128)(2,1)S(1)} %get-tuple-element.22), channel_id=1, source_target_pairs={{0,48},{8,56},{16,32},{24,40},{32,16},{40,24},{48,0},{56,8},{64,11... | collective-permute-start | bytes 442376 | tf_op jit(solution)/shard_map/ppermute | solution.py:37
  23.4 11.5 %collective-permute-start.16 = (f32[2,64,128]{2,1,0:T(8,128)S(1)}, f32[2,64,128]{2,1,0:T(8,128)S(1)}, u32[]{:S(2)}, u32[]{:S(2)}) collective-permute-start(f32[2,64,128]{2,1,0:T(8,128)S(1)} %pad_maximum_fusion), channel_id=1, source_target_pairs={{0,2},{1,3},{2,0},{3,1},{4,6},{5,7},{6,4},{7,5},{8,10},{9,11},{10,... | collective-permute-start | bytes 196616 | tf_op jit(solution)/shard_map/ppermute | solution.py:37
  26.3 0.8 copy-start
  27.1 1.7 %collective-permute-start.3 = (f32[256,128]{1,0:T(8,128)S(1)}, f32[256,128]{1,0:T(8,128)S(1)}, u32[]{:S(2)}, u32[]{:S(2)}) collective-permute-start(f32[256,128]{1,0:T(8,128)S(1)} %shard_map.103.own), channel_id=1, source_target_pairs={{0,8},{8,0},{16,24},{24,16},{32,40},{40,32},{48,56},{56,48},{64,72... | collective-permute-start | bytes 393224 | tf_op jit(solution)/shard_map/ppermute | solution.py:37
  27.2 15.5 %collective-permute-start.17 = (f32[2,64,128]{2,1,0:T(8,128)S(1)}, f32[2,64,128]{2,1,0:T(8,128)S(1)}, u32[]{:S(2)}, u32[]{:S(2)}) collective-permute-start(f32[2,64,128]{2,1,0:T(8,128)S(1)} %pad_maximum_fusion), channel_id=1, source_target_pairs={{0,3},{1,2},{2,1},{3,0},{4,7},{5,6},{6,5},{7,4},{8,11},{9,10},{10,... | collective-permute-start | bytes 196616 | tf_op jit(solution)/shard_map/ppermute | solution.py:37
  31.0 4.8 %collective-permute-start.7 = (f32[32,512]{1,0:T(8,128)S(1)}, f32[32,512]{1,0:T(8,128)S(1)}, u32[]{:S(2)}, u32[]{:S(2)}) collective-permute-start(f32[32,512]{1,0:T(8,128)S(1)} %shard_map.106.after.part), channel_id=1, source_target_pairs={{0,16},{8,24},{16,0},{24,8},{32,48},{40,56},{48,32},{56,40},{64,80... | collective-permute-start | bytes 196616 | tf_op jit(solution)/shard_map/ppermute | solution.py:37
  33.3 5.9 %collective-permute-start.8 = (f32[32,512]{1,0:T(8,128)S(1)}, f32[32,512]{1,0:T(8,128)S(1)}, u32[]{:S(2)}, u32[]{:S(2)}) collective-permute-start(f32[32,512]{1,0:T(8,128)S(1)} %shard_map.106.after.part), channel_id=1, source_target_pairs={{0,32},{8,40},{16,48},{24,56},{32,0},{40,8},{48,16},{56,24},{64,96... | collective-permute-start | bytes 196616 | tf_op jit(solution)/shard_map/ppermute | solution.py:37
  34.3 5.1 %collective-permute-start.9 = (f32[32,512]{1,0:T(8,128)S(1)}, f32[32,512]{1,0:T(8,128)S(1)}, u32[]{:S(2)}, u32[]{:S(2)}) collective-permute-start(f32[32,512]{1,0:T(8,128)S(1)} %shard_map.106.after.part), channel_id=1, source_target_pairs={{0,48},{8,56},{16,32},{24,40},{32,16},{40,24},{48,0},{56,8},{64,11... | collective-permute-start | bytes 196616 | tf_op jit(solution)/shard_map/ppermute | solution.py:37
  35.8 18.2 %copy-start.1 = (f32[1,8,1024]{2,1,0:T(8,128)S(1)}, f32[1,8,1024]{2,1,0:T(8,128)}, u32[]{:S(2)}) copy-start(f32[1,8,1024]{2,1,0:T(8,128)} %param.11) | copy-start | bytes 98308
  35.8 18.2 %copy-start.5 = (f32[1,8,1024]{2,1,0:T(8,128)S(1)}, f32[1,8,1024]{2,1,0:T(8,128)}, u32[]{:S(2)}) copy-start(f32[1,8,1024]{2,1,0:T(8,128)} %param.12) | copy-start | bytes 98308
  42.4 1.6 %collective-permute-start.10 = (f32[256,128]{1,0:T(8,128)S(1)}, f32[256,128]{1,0:T(8,128)S(1)}, u32[]{:S(2)}, u32[]{:S(2)}) collective-permute-start(f32[256,128]{1,0:T(8,128)S(1)} %get-tuple-element.24), channel_id=1, source_target_pairs={{0,8},{8,0},{16,24},{24,16},{32,40},{40,32},{48,56},{56,48},{64,72... | collective-permute-start | bytes 393224 | tf_op jit(solution)/shard_map/ppermute | solution.py:37
  44.1 4.6 %collective-permute-start.11 = (f32[64,128]{1,0:T(8,128)S(1)}, f32[64,128]{1,0:T(8,128)S(1)}, u32[]{:S(2)}, u32[]{:S(2)}) collective-permute-start(f32[64,128]{1,0:T(8,128)S(1)} %get-tuple-element.46), channel_id=1, source_target_pairs={{0,64},{8,72},{16,80},{24,88},{32,96},{40,104},{48,112},{56,120},{... | collective-permute-start | bytes 98312 | tf_op jit(solution)/shard_map/ppermute | solution.py:37
  44.3 5.9 %collective-permute-start.12 = (f32[64,128]{1,0:T(8,128)S(1)}, f32[64,128]{1,0:T(8,128)S(1)}, u32[]{:S(2)}, u32[]{:S(2)}) collective-permute-start(f32[64,128]{1,0:T(8,128)S(1)} %get-tuple-element.45), channel_id=1, source_target_pairs={{0,128},{8,136},{16,144},{24,152},{32,160},{40,168},{48,176},{56,1... | collective-permute-start | bytes 98312 | tf_op jit(solution)/shard_map/ppermute | solution.py:37
  48.3 5.7 %collective-permute-start.13 = (f32[64,128]{1,0:T(8,128)S(1)}, f32[64,128]{1,0:T(8,128)S(1)}, u32[]{:S(2)}, u32[]{:S(2)}) collective-permute-start(f32[64,128]{1,0:T(8,128)S(1)} %get-tuple-element.44), channel_id=1, source_target_pairs={{0,192},{8,200},{16,208},{24,216},{32,224},{40,232},{48,240},{56,2... | collective-permute-start | bytes 98312 | tf_op jit(solution)/shard_map/ppermute | solution.py:37
  54.1 4.4 %collective-permute-start.18 = (f32[64,128]{1,0:T(8,128)S(1)}, f32[64,128]{1,0:T(8,128)S(1)}, u32[]{:S(2)}, u32[]{:S(2)}) collective-permute-start(f32[64,128]{1,0:T(8,128)S(1)} %fusion.5.a), channel_id=1, source_target_pairs={{0,64},{8,72},{16,80},{24,88},{32,96},{40,104},{48,112},{56,120},{... | collective-permute-start | bytes 98312 | tf_op jit(solution)/shard_map/ppermute | solution.py:37
  54.1 4.9 %collective-permute-start.19 = (f32[64,128]{1,0:T(8,128)S(1)}, f32[64,128]{1,0:T(8,128)S(1)}, u32[]{:S(2)}, u32[]{:S(2)}) collective-permute-start(f32[64,128]{1,0:T(8,128)S(1)} %fusion.5.a), channel_id=1, source_target_pairs={{0,128},{8,136},{16,144},{24,152},{32,160},{40,168},{48,176},{56,1... | collective-permute-start | bytes 98312 | tf_op jit(solution)/shard_map/ppermute | solution.py:37
  55.1 5.7 %collective-permute-start.20 = (f32[64,128]{1,0:T(8,128)S(1)}, f32[64,128]{1,0:T(8,128)S(1)}, u32[]{:S(2)}, u32[]{:S(2)}) collective-permute-start(f32[64,128]{1,0:T(8,128)S(1)} %fusion.5.a), channel_id=1, source_target_pairs={{0,192},{8,200},{16,208},{24,216},{32,224},{40,232},{48,240},{56,2... | collective-permute-start | bytes 98312 | tf_op jit(solution)/shard_map/ppermute | solution.py:37
  60.8 1.4 %collective-permute-start.21 = (f32[256,128]{1,0:T(8,128)S(1)}, f32[256,128]{1,0:T(8,128)S(1)}, u32[]{:S(2)}, u32[]{:S(2)}) collective-permute-start(f32[256,128]{1,0:T(8,128)S(1)} %shard_map.109.own), channel_id=1, source_target_pairs={{0,8},{8,0},{16,24},{24,16},{32,40},{40,32},{48,56},{56,48},{64,72... | collective-permute-start | bytes 393224 | tf_op jit(solution)/shard_map/ppermute | solution.py:37
  62.3 5.9 %collective-permute-start.22 = (f32[8,128]{1,0:T(8,128)S(1)}, f32[8,128]{1,0:T(8,128)S(1)}, u32[]{:S(2)}, u32[]{:S(2)}) collective-permute-start(f32[8,128]{1,0:T(8,128)S(1)} %bitcast_reduce_fusion.refs_2_), channel_id=1, source_target_pairs={{0,16},{8,24},{16,0},{24,8},{32,48},{40,56},{48,32},{56,40},{64,80... | collective-permute-start | bytes 12296 | tf_op jit(solution)/shard_map/ppermute | solution.py:37
  65.2 5.1 %collective-permute-start.23 = (f32[8,128]{1,0:T(8,128)S(1)}, f32[8,128]{1,0:T(8,128)S(1)}, u32[]{:S(2)}, u32[]{:S(2)}) collective-permute-start(f32[8,128]{1,0:T(8,128)S(1)} %bitcast_reduce_fusion.refs_2_), channel_id=1, source_target_pairs={{0,32},{8,40},{16,48},{24,56},{32,0},{40,8},{48,16},{56,24},{64,96... | collective-permute-start | bytes 12296 | tf_op jit(solution)/shard_map/ppermute | solution.py:37
  65.4 4.9 %collective-permute-start.24 = (f32[8,128]{1,0:T(8,128)S(1)}, f32[8,128]{1,0:T(8,128)S(1)}, u32[]{:S(2)}, u32[]{:S(2)}) collective-permute-start(f32[8,128]{1,0:T(8,128)S(1)} %bitcast_reduce_fusion.refs_2_), channel_id=1, source_target_pairs={{0,48},{8,56},{16,32},{24,40},{32,16},{40,24},{48,0},{56,8},{64,11... | collective-permute-start | bytes 12296 | tf_op jit(solution)/shard_map/ppermute | solution.py:37
  72.5 9.8 %collective-permute-start.32 = (f32[64,128]{1,0:T(8,128)S(1)}, f32[64,128]{1,0:T(8,128)S(1)}, u32[]{:S(2)}, u32[]{:S(2)}) collective-permute-start(f32[64,128]{1,0:T(8,128)S(1)} %get-tuple-element.39), channel_id=1, source_target_pairs={{0,4},{4,0},{1,5},{5,1},{2,6},{6,2},{3,7},{7,3},{8,12},{12,8},{9,1... | collective-permute-start | bytes 98312 | tf_op jit(solution)/shard_map/ppermute | solution.py:37
  78.4 8.6 %collective-permute-start.25 = (f32[32,512]{1,0:T(8,128)S(1)}, f32[32,512]{1,0:T(8,128)S(1)}, u32[]{:S(2)}, u32[]{:S(2)}) collective-permute-start(f32[32,512]{1,0:T(8,128)S(1)} %get-tuple-element.25.after.part), channel_id=1, source_target_pairs={{0,16},{8,24},{16,0},{24,8},{32,48},{40,56},{48,32},{56,40},{64,80... | collective-permute-start | bytes 196616 | tf_op jit(solution)/shard_map/ppermute | solution.py:37
  80.8 7.2 %collective-permute-start.26 = (f32[32,512]{1,0:T(8,128)S(1)}, f32[32,512]{1,0:T(8,128)S(1)}, u32[]{:S(2)}, u32[]{:S(2)}) collective-permute-start(f32[32,512]{1,0:T(8,128)S(1)} %get-tuple-element.25.after.part), channel_id=1, source_target_pairs={{0,32},{8,40},{16,48},{24,56},{32,0},{40,8},{48,16},{56,24},{64,96... | collective-permute-start | bytes 196616 | tf_op jit(solution)/shard_map/ppermute | solution.py:37
  81.6 6.4 %collective-permute-start.27 = (f32[32,512]{1,0:T(8,128)S(1)}, f32[32,512]{1,0:T(8,128)S(1)}, u32[]{:S(2)}, u32[]{:S(2)}) collective-permute-start(f32[32,512]{1,0:T(8,128)S(1)} %get-tuple-element.25.after.part), channel_id=1, source_target_pairs={{0,48},{8,56},{16,32},{24,40},{32,16},{40,24},{48,0},{56,8},{64,11... | collective-permute-start | bytes 196616 | tf_op jit(solution)/shard_map/ppermute | solution.py:37
  82.3 8.9 %collective-permute-start.33 = (f32[2,64,128]{2,1,0:T(8,128)S(1)}, f32[2,64,128]{2,1,0:T(8,128)S(1)}, u32[]{:S(2)}, u32[]{:S(2)}) collective-permute-start(f32[2,64,128]{2,1,0:T(8,128)S(1)} %pad_maximum_fusion.1), channel_id=1, source_target_pairs={{0,1},{1,0},{2,3},{3,2},{4,5},{5,4},{6,7},{7,6},{8,9},{9,8},{10,11... | collective-permute-start | bytes 196616 | tf_op jit(solution)/shard_map/ppermute | solution.py:37
  83.7 7.5 %collective-permute-start.34 = (f32[2,64,128]{2,1,0:T(8,128)S(1)}, f32[2,64,128]{2,1,0:T(8,128)S(1)}, u32[]{:S(2)}, u32[]{:S(2)}) collective-permute-start(f32[2,64,128]{2,1,0:T(8,128)S(1)} %pad_maximum_fusion.1), channel_id=1, source_target_pairs={{0,2},{1,3},{2,0},{3,1},{4,6},{5,7},{6,4},{7,5},{8,10},{9,11},{10,... | collective-permute-start | bytes 196616 | tf_op jit(solution)/shard_map/ppermute | solution.py:37
  87.0 5.5 %collective-permute-start.35 = (f32[2,64,128]{2,1,0:T(8,128)S(1)}, f32[2,64,128]{2,1,0:T(8,128)S(1)}, u32[]{:S(2)}, u32[]{:S(2)}) collective-permute-start(f32[2,64,128]{2,1,0:T(8,128)S(1)} %pad_maximum_fusion.1), channel_id=1, source_target_pairs={{0,3},{1,2},{2,1},{3,0},{4,7},{5,6},{6,5},{7,4},{8,11},{9,10},{10,... | collective-permute-start | bytes 196616 | tf_op jit(solution)/shard_map/ppermute | solution.py:37
  91.1 1.5 %collective-permute-start.28 = (f32[256,128]{1,0:T(8,128)S(1)}, f32[256,128]{1,0:T(8,128)S(1)}, u32[]{:S(2)}, u32[]{:S(2)}) collective-permute-start(f32[256,128]{1,0:T(8,128)S(1)} %get-tuple-element.28), channel_id=1, source_target_pairs={{0,8},{8,0},{16,24},{24,16},{32,40},{40,32},{48,56},{56,48},{64,72... | collective-permute-start | bytes 393224 | tf_op jit(solution)/shard_map/ppermute | solution.py:37
  92.7 4.6 %collective-permute-start.29 = (f32[64,128]{1,0:T(8,128)S(1)}, f32[64,128]{1,0:T(8,128)S(1)}, u32[]{:S(2)}, u32[]{:S(2)}) collective-permute-start(f32[64,128]{1,0:T(8,128)S(1)} %get-tuple-element.41), channel_id=1, source_target_pairs={{0,64},{8,72},{16,80},{24,88},{32,96},{40,104},{48,112},{56,120},{... | collective-permute-start | bytes 98312 | tf_op jit(solution)/shard_map/ppermute | solution.py:37
  92.8 5.4 %collective-permute-start.30 = (f32[64,128]{1,0:T(8,128)S(1)}, f32[64,128]{1,0:T(8,128)S(1)}, u32[]{:S(2)}, u32[]{:S(2)}) collective-permute-start(f32[64,128]{1,0:T(8,128)S(1)} %get-tuple-element.43), channel_id=1, source_target_pairs={{0,128},{8,136},{16,144},{24,152},{32,160},{40,168},{48,176},{56,1... | collective-permute-start | bytes 98312 | tf_op jit(solution)/shard_map/ppermute | solution.py:37
  95.2 5.7 %collective-permute-start.31 = (f32[64,128]{1,0:T(8,128)S(1)}, f32[64,128]{1,0:T(8,128)S(1)}, u32[]{:S(2)}, u32[]{:S(2)}) collective-permute-start(f32[64,128]{1,0:T(8,128)S(1)} %get-tuple-element.42), channel_id=1, source_target_pairs={{0,192},{8,200},{16,208},{24,216},{32,224},{40,232},{48,240},{56,2... | collective-permute-start | bytes 98312 | tf_op jit(solution)/shard_map/ppermute | solution.py:37
  101.0 13.1 %collective-permute-start.36 = (f32[2,64,128]{2,1,0:T(8,128)S(1)}, f32[2,64,128]{2,1,0:T(8,128)S(1)}, u32[]{:S(2)}, u32[]{:S(2)}) collective-permute-start(f32[2,64,128]{2,1,0:T(8,128)S(1)} %pad_maximum_fusion.2), channel_id=1, source_target_pairs={{0,4},{4,0},{1,5},{5,1},{2,6},{6,2},{3,7},{7,3},{8,12},{12,8},{9,1... | collective-permute-start | bytes 196616 | tf_op jit(solution)/shard_map/ppermute | solution.py:37
  105.5 17.0 %all-to-all-start = ((f32[64,1,128]{2,1,0:T(1,128)}), f32[64,1,128]{2,1,0:T(1,128)S(1)}, u32[]{:S(2)}, u32[]{:S(2)}) async-start(f32[64,1,128]{2,1,0:T(1,128)} %bitcast.43), calls=%async_computation | async-start | bytes 65536 | tf_op jit(solution)/shard_map/all_to_all | solution.py:382
  122.7 5.0 %collective-permute-start.37 = (f32[128,128]{1,0:T(8,128)S(1)}, f32[128,128]{1,0:T(8,128)S(1)}, u32[]{:S(2)}, u32[]{:S(2)}) collective-permute-start(f32[128,128]{1,0:T(8,128)S(1)} %get-tuple-element.30.near0), channel_id=1, source_target_pairs={{0,1},{1,0},{2,3},{3,2},{4,5},{5,4},{6,7},{7,6},{8,9},{9,8},{10,11... | collective-permute-start | bytes 196616 | tf_op jit(solution)/shard_map/ppermute | solution.py:37
  122.8 6.8 %collective-permute-start.38 = (f32[128,128]{1,0:T(8,128)S(1)}, f32[128,128]{1,0:T(8,128)S(1)}, u32[]{:S(2)}, u32[]{:S(2)}) collective-permute-start(f32[128,128]{1,0:T(8,128)S(1)} %get-tuple-element.30.near0), channel_id=1, source_target_pairs={{0,2},{1,3},{2,0},{3,1},{4,6},{5,7},{6,4},{7,5},{8,10},{9,11},{10,... | collective-permute-start | bytes 196616 | tf_op jit(solution)/shard_map/ppermute | solution.py:37
  126.3 5.5 %collective-permute-start.39 = (f32[128,128]{1,0:T(8,128)S(1)}, f32[128,128]{1,0:T(8,128)S(1)}, u32[]{:S(2)}, u32[]{:S(2)}) collective-permute-start(f32[128,128]{1,0:T(8,128)S(1)} %get-tuple-element.30.near0), channel_id=1, source_target_pairs={{0,3},{1,2},{2,1},{3,0},{4,7},{5,6},{6,5},{7,4},{8,11},{9,10},{10,... | collective-permute-start | bytes 196616 | tf_op jit(solution)/shard_map/ppermute | solution.py:37
